TPU v7x, 32 devices: a whole 2x2x4 slice. The times are simulated.
32 devices in a mesh: row: 8 (over z, y), col: 4 (over x, core).
Axes of the slice: x: 2, y: 2, z: 4, core: 2. Of those that a mesh axis runs over, the one named last changes fastest.
Arguments:
- tokens: bfloat16 [16, 2048, 768], P('row', 'col'), may hold values from -6 to 6
- segment_ids: int32 [16, 2048], P('row', 'col'), may hold values from 0 to 1, never falling along the last dimension, each value on 1 to 2000 neighbouring positions
- in_weight: bfloat16 [768, 2304], P('row', 'col'), may hold values from -0.21875 to 0.21875
- in_bias: bfloat16 [2304], replicated, may hold values from -3 to 3
- mix_weight: bfloat16 [768, 768], P('row', 'col'), may hold values from -1.5 to 1.5
- mix_bias: bfloat16 [768], replicated, may hold values from -3 to 3
- first_gain: bfloat16 [768], replicated, may hold values from 0.25 to 1.75
- first_shift: bfloat16 [768], replicated, may hold values from -3 to 3
- up_weight: bfloat16 [768, 3072], P('row', 'col'), may hold values from -0.21875 to 0.21875
- up_bias: bfloat16 [3072], replicated, may hold values from -3 to 3
- down_weight: bfloat16 [3072, 768], P('row', 'col'), may hold values from -0.109375 to 0.109375
- down_bias: bfloat16 [768], replicated, may hold values from -3 to 3
- second_gain: bfloat16 [768], replicated, may hold values from 0.25 to 1.75
- second_shift: bfloat16 [768], replicated, may hold values from -3 to 3
- cotangent: float32 [16, 2048, 768], P('row', 'col'), may hold values from -6 to 6
Outputs:
- layer_out: bfloat16 [16, 2048, 768], P('row', 'col')
- tokens_grad: float32 [16, 2048, 768], P('row', 'col')
- in_weight_grad: float32 [768, 2304], P('row', 'col')
- in_bias_grad: float32 [2304], replicated
- mix_weight_grad: float32 [768, 768], P('row', 'col')
- mix_bias_grad: float32 [768], replicated
- first_gain_grad: float32 [768], replicated
- first_shift_grad: float32 [768], replicated
- up_weight_grad: float32 [768, 3072], P('row', 'col')
- up_bias_grad: float32 [3072], replicated
- down_weight_grad: float32 [3072, 768], P('row', 'col')
- down_bias_grad: float32 [768], replicated
- second_gain_grad: float32 [768], replicated
- second_shift_grad: float32 [768], replicated
Inputs may be any that keep to these rules, and one draw needn't show every extreme that they name: `segment_ids`: in each sequence 2 documents numbered from 0 in order of position; each covers 1 to 2000 consecutive positions.
All inputs are finite; a program needn't handle non-finite values.
Results may differ from a plain program's by a relative error of at most 0.019.
Values may be sent and summed in bfloat16 or wider, within the bound.
A program may use at most 256 MiB of HBM per device.

v0:
```python
import math

import jax
import jax.numpy as jnp
from jax import lax
from jax.sharding import PartitionSpec as P

HEADS = 12
HEAD_DIM = 64
DOC_MAX = 2000


EPSILON = 1e-05
FLOOR = 4.0
PRECISE = lax.Precision.HIGHEST


def prefix(value, axis, join, neutral):
    count, mine = (lax.axis_size(axis), lax.axis_index(axis))
    pieces = jax.tree.map(lambda part: lax.all_gather(part, axis), value)
    total = jax.tree.map(
        lambda part, zero: jnp.full_like(part, 0) + jnp.asarray(zero, part.dtype), value, neutral
    )

    def hop(position, total):
        longer = join(total, jax.tree.map(lambda part: part[position], pieces))
        return jax.tree.map(lambda new, old: jnp.where(position < mine, new, old), longer, total)

    return lax.fori_loop(0, count - 1, hop, total)


def entering(shard, axis, join, neutral):
    count = lax.axis_size(axis)
    place = lax.axis_index(axis)
    ahead = count - 1 - place
    gathered = jax.tree.map(
        lambda a, kind: lax.all_gather(a.astype(kind), axis),
        shard,
        jax.tree.map(lambda a: jnp.bfloat16 if a.dtype == jnp.float32 else a.dtype, shard),
    )
    state = jax.tree.map(lambda a, e: jnp.zeros_like(a) + jnp.asarray(e, a.dtype), shard, neutral)

    def one(hop, state):
        source = count - 1 - hop
        return join(
            state,
            jax.tree.map(
                lambda a, own: lax.dynamic_index_in_dim(a, source, 0, False).astype(own.dtype),
                gathered,
                shard,
            ),
        )

    return lax.fori_loop(0, ahead, one, state)


def layer_norm(values, gain_vec, shift_vec):
    center = values - jnp.mean(values, axis=-1, keepdims=True)
    spread = jnp.mean(center * center, axis=-1, keepdims=True)
    return center * lax.rsqrt(spread + EPSILON) * gain_vec + shift_vec


def gelu_exact(values):
    return jax.nn.gelu(values, approximate=False)


def left_product(first, second):
    return lax.dot_general(
        first, second, (((0,), (0,)), ((), ())), preferred_element_type=jnp.float32
    )


def right_product(first, second):
    return lax.dot_general(
        first, second, (((1,), (1,)), ((), ())), preferred_element_type=jnp.float32
    )


def join_offsets(earlier, later):
    early_first, early_last, early_run = earlier
    late_first, late_last, late_run = later
    passes = (late_last < 0) | (late_first == late_last) & (late_first == early_last)
    first_id = jnp.where(early_first < 0, late_first, early_first)
    last_id = jnp.where(late_last < 0, early_last, late_last)
    return (first_id, last_id, late_run + jnp.where(passes, early_run, 0))


def join_states(earlier, later):
    early_first, early_last, early_state, early_total = earlier
    late_first, late_last, late_state, late_total = later
    passes = (late_last < 0.0) | (late_first == late_last) & (late_first == early_last)
    first_id = jnp.where(early_first < 0.0, late_first, early_first)
    last_id = jnp.where(late_last < 0.0, early_last, late_last)
    state_sum = late_state + jnp.where(passes[None, :, None, None], early_state, 0.0)
    total_sum = late_total + jnp.where(passes[None, :, None], early_total, 0.0)
    return (first_id, last_id, state_sum, total_sum)


def join_grads(earlier, later):
    high_first, high_last, high_state, high_total = earlier
    lower_first, lower_last, lower_state, lower_total = later
    passes = (lower_first < 0.0) | (lower_first == lower_last) & (high_first == lower_last)
    first_id = jnp.where(lower_first < 0.0, high_first, lower_first)
    last_id = jnp.where(high_last < 0.0, lower_last, high_last)
    state_sum = lower_state + jnp.where(passes[None, :, None, None], high_state, 0.0)
    total_sum = lower_total + jnp.where(passes[None, :, None], high_total, 0.0)
    return (first_id, last_id, state_sum, total_sum)


def fetch_weights(in_weight, mix_weight, up_weight, down_weight):
    partial_value = (
        lax.all_gather(in_weight, "col", axis=1, tiled=True),
        lax.all_gather(mix_weight, "col", axis=1, tiled=True),
        lax.all_gather(up_weight, "col", axis=1, tiled=True),
        lax.all_gather(down_weight, "col", axis=1, tiled=True),
    )
    result = (
        lax.all_gather(partial_value[0], "row", axis=0, tiled=True),
        lax.all_gather(partial_value[1], "row", axis=0, tiled=True),
        lax.all_gather(partial_value[2], "row", axis=0, tiled=True),
        lax.all_gather(partial_value[3], "row", axis=0, tiled=True),
    )
    return result


def reduce_weights(in_grad, mix_grad, up_grad, down_grad):
    partial_value = (
        lax.psum_scatter(
            in_grad.astype(jnp.bfloat16), "col", scatter_dimension=1, tiled=True
        ).astype(jnp.float32),
        lax.psum_scatter(
            mix_grad.astype(jnp.bfloat16), "col", scatter_dimension=1, tiled=True
        ).astype(jnp.float32),
        lax.psum_scatter(
            up_grad.astype(jnp.bfloat16), "col", scatter_dimension=1, tiled=True
        ).astype(jnp.float32),
        lax.psum_scatter(
            down_grad.astype(jnp.bfloat16), "col", scatter_dimension=1, tiled=True
        ).astype(jnp.float32),
    )
    result = (
        lax.psum_scatter(
            partial_value[0].astype(jnp.bfloat16), "row", scatter_dimension=0, tiled=True
        ).astype(jnp.float32),
        lax.psum_scatter(
            partial_value[1].astype(jnp.bfloat16), "row", scatter_dimension=0, tiled=True
        ).astype(jnp.float32),
        lax.psum_scatter(
            partial_value[2].astype(jnp.bfloat16), "row", scatter_dimension=0, tiled=True
        ).astype(jnp.float32),
        lax.psum_scatter(
            partial_value[3].astype(jnp.bfloat16), "row", scatter_dimension=0, tiled=True
        ).astype(jnp.float32),
    )
    return result


def features(pre_act, cosine, sine_part):
    active = jax.nn.relu(pre_act)
    return jnp.concatenate([active * cosine, active * sine_part], axis=-1).astype(jnp.bfloat16)


def by_head(values, seq_count, length):
    return values.reshape(seq_count, length, values.shape[1], values.shape[2]).transpose(2, 0, 1, 3)


def to_rows(values):
    return values.transpose(1, 2, 0, 3).reshape(
        values.shape[1] * values.shape[2], values.shape[0], values.shape[3]
    )


def per_device(
    tokens,
    segment_ids,
    in_weight,
    in_bias,
    mix_weight,
    mix_bias,
    first_gain,
    first_shift,
    up_weight,
    up_bias,
    down_weight,
    down_bias,
    second_gain,
    second_shift,
    cotangent,
):
    seq_count, length, model_width = tokens.shape
    row_total = seq_count * length
    head_count = HEADS
    head_size = HEAD_DIM
    indices = jnp.arange(length, dtype=jnp.int32)
    fresh_doc = jnp.concatenate(
        [jnp.ones((seq_count, 1), jnp.bool_), segment_ids[:, 1:] != segment_ids[:, :-1]], axis=1
    )
    doc_starts = lax.cummax(jnp.where(fresh_doc, indices[None, :], 0), axis=1)
    first_ids = segment_ids[:, 0]
    last_ids = segment_ids[:, -1]
    last_mask = segment_ids == last_ids[:, None]
    first_mask = segment_ids == first_ids[:, None]
    run_length = jnp.sum(last_mask.astype(jnp.int32), axis=1)
    negative = jnp.full((seq_count,), -1, jnp.int32)
    offsets = prefix(
        (first_ids, last_ids, run_length),
        "col",
        join_offsets,
        (negative, negative, jnp.zeros((seq_count,), jnp.int32)),
    )
    continues = segment_ids == offsets[1][:, None]
    positions = indices[None, :] - doc_starts + jnp.where(continues, offsets[2][:, None], 0)
    full_in, full_mix, full_up, full_down = fetch_weights(
        in_weight, mix_weight, up_weight, down_weight
    )
    flat_tokens = tokens.reshape(row_total, model_width)
    projected = jnp.dot(flat_tokens, full_in, preferred_element_type=jnp.float32) + in_bias.astype(
        jnp.float32
    )
    angles = positions.reshape(row_total).astype(jnp.float32) * (math.pi / (2.0 * DOC_MAX))
    cosine = jnp.cos(angles)[:, None, None]
    sine_part = jnp.sin(angles)[:, None, None]
    query_pre = projected[:, :model_width].reshape(row_total, head_count, head_size)
    key_pre = projected[:, model_width : 2 * model_width].reshape(row_total, head_count, head_size)
    value_low = (
        projected[:, 2 * model_width :]
        .astype(jnp.bfloat16)
        .reshape(row_total, head_count, head_size)
    )
    query_heads = by_head(features(query_pre, cosine, sine_part), seq_count, length)
    key_heads = by_head(features(key_pre, cosine, sine_part), seq_count, length)
    value_heads = by_head(value_low, seq_count, length)
    last_low = last_mask.astype(jnp.bfloat16)[None, :, :, None]
    key_last = key_heads * last_low
    local_state = jnp.einsum(
        "hsnf,hsnd->hsfd", key_last, value_heads, preferred_element_type=jnp.float32
    )
    local_total = jnp.sum(key_last.astype(jnp.float32), axis=2)
    first_float = first_ids.astype(jnp.float32)
    last_float = last_ids.astype(jnp.float32)
    empty_ids = jnp.full((seq_count,), -1.0, jnp.float32)
    carried = prefix(
        (first_float, last_float, local_state, local_total),
        "col",
        join_states,
        (empty_ids, empty_ids, jnp.zeros_like(local_state), jnp.zeros_like(local_total)),
    )
    same_doc = segment_ids[:, :, None] == segment_ids[:, None, :]
    causal = indices[None, :] <= indices[:, None]
    score_mask = (same_doc & causal[None]).astype(jnp.float32)
    mask_low = score_mask.astype(jnp.bfloat16)
    carry_float = continues.astype(jnp.float32)
    last_weight = last_mask.astype(jnp.float32)

    def head_forward(inputs):
        query_head, key_head, value_head, state_head, total_head = inputs
        scores = (
            jnp.einsum("sif,sjf->sij", query_head, key_head, preferred_element_type=jnp.float32)
            * score_mask
        )
        query_wide = query_head.astype(jnp.float32)
        numerator = jnp.einsum(
            "sij,sjd->sid",
            scores.astype(jnp.bfloat16),
            value_head,
            preferred_element_type=jnp.float32,
        )
        numerator = numerator + carry_float[:, :, None] * jnp.einsum(
            "sif,sfd->sid", query_wide, state_head, precision=PRECISE
        )
        denominator = jnp.sum(scores, axis=-1) + carry_float * jnp.einsum(
            "sif,sf->si", query_wide, total_head, precision=PRECISE
        )
        return (numerator / jnp.maximum(denominator, FLOOR)[:, :, None], denominator)

    attended, denominators = lax.map(
        head_forward, (query_heads, key_heads, value_heads, carried[2], carried[3])
    )
    attended_low = to_rows(attended).reshape(row_total, model_width).astype(jnp.bfloat16)
    mixed_out = jnp.dot(
        attended_low, full_mix, preferred_element_type=jnp.float32
    ) + mix_bias.astype(jnp.float32)
    pre_sum = flat_tokens.astype(jnp.float32) + mixed_out
    hidden, first_pull = jax.vjp(
        layer_norm, pre_sum, first_gain.astype(jnp.float32), first_shift.astype(jnp.float32)
    )
    hidden_low = hidden.astype(jnp.bfloat16)
    up_proj = jnp.dot(hidden_low, full_up, preferred_element_type=jnp.float32) + up_bias.astype(
        jnp.float32
    )
    activated, gelu_pull = jax.vjp(gelu_exact, up_proj)
    act_low = activated.astype(jnp.bfloat16)
    down_proj = jnp.dot(act_low, full_down, preferred_element_type=jnp.float32) + down_bias.astype(
        jnp.float32
    )
    result, second_pull = jax.vjp(
        layer_norm,
        hidden + down_proj,
        second_gain.astype(jnp.float32),
        second_shift.astype(jnp.float32),
    )
    layer_out = result.astype(jnp.bfloat16).reshape(seq_count, length, model_width)
    back_in, back_mix, back_up, back_down = fetch_weights(
        in_weight, mix_weight, up_weight, down_weight
    )
    sum_grad, second_gain_grad, second_shift_grad = second_pull(
        cotangent.reshape(row_total, model_width)
    )
    down_grad = sum_grad.astype(jnp.bfloat16)
    down_weight_grad = left_product(act_low, down_grad)
    down_bias_grad = jnp.sum(down_grad.astype(jnp.float32), axis=0)
    up_grad = gelu_pull(right_product(down_grad, back_down))[0].astype(jnp.bfloat16)
    up_weight_grad = left_product(hidden_low, up_grad)
    up_bias_grad = jnp.sum(up_grad.astype(jnp.float32), axis=0)
    hidden_grad = sum_grad + right_product(up_grad, back_up)
    pre_grad, first_gain_grad, first_shift_grad = first_pull(hidden_grad)
    mixed_grad = pre_grad.astype(jnp.bfloat16)
    mix_weight_grad = left_product(attended_low, mixed_grad)
    mix_bias_grad = jnp.sum(mixed_grad.astype(jnp.float32), axis=0)
    attended_grad = by_head(
        right_product(mixed_grad, back_mix).reshape(row_total, head_count, head_size),
        seq_count,
        length,
    )
    floored = jnp.maximum(denominators, FLOOR)
    numerator_grad = (attended_grad / floored[..., None]).astype(jnp.bfloat16)
    denominator_grad = (
        -jnp.sum(attended_grad * attended, axis=-1)
        / floored
        * (denominators > FLOOR).astype(jnp.float32)
    )
    query_first = query_heads * first_mask.astype(jnp.bfloat16)[None, :, :, None]
    state_terms = jnp.einsum(
        "hsif,hsid->hsfd", query_first, numerator_grad, preferred_element_type=jnp.float32
    )
    total_terms = jnp.einsum(
        "hsif,hsi->hsf", query_first.astype(jnp.float32), denominator_grad, precision=PRECISE
    )
    later = entering(
        (first_float, last_float, state_terms, total_terms),
        "col",
        join_grads,
        (empty_ids, empty_ids, jnp.zeros_like(state_terms), jnp.zeros_like(total_terms)),
    )
    follows = (later[0] == last_float).astype(jnp.float32)
    state_next = later[2] * follows[None, :, None, None]
    total_next = later[3] * follows[None, :, None]

    def head_backward(inputs):
        (
            query_head,
            key_head,
            value_head,
            state_head,
            total_head,
            numer_grad,
            denom_grad,
            next_state,
            next_total,
        ) = inputs
        scores = (
            jnp.einsum("sif,sjf->sij", query_head, key_head, preferred_element_type=jnp.float32)
            * score_mask
        )
        score_grad = (
            jnp.einsum("sid,sjd->sij", numer_grad, value_head, preferred_element_type=jnp.float32)
            + denom_grad[:, :, None]
        )
        score_grad = score_grad.astype(jnp.bfloat16) * mask_low
        query_grad = jnp.einsum(
            "sij,sjf->sif", score_grad, key_head, preferred_element_type=jnp.float32
        )
        query_grad = query_grad + carry_float[:, :, None] * (
            jnp.einsum(
                "sid,sfd->sif", numer_grad.astype(jnp.float32), state_head, precision=PRECISE
            )
            + denom_grad[:, :, None] * total_head[:, None, :]
        )
        key_grad = jnp.einsum(
            "sij,sif->sjf", score_grad, query_head, preferred_element_type=jnp.float32
        )
        key_grad = key_grad + last_weight[:, :, None] * (
            jnp.einsum(
                "sjd,sfd->sjf", value_head.astype(jnp.float32), next_state, precision=PRECISE
            )
            + next_total[:, None, :]
        )
        value_grad = jnp.einsum(
            "sij,sid->sjd",
            scores.astype(jnp.bfloat16),
            numer_grad,
            preferred_element_type=jnp.float32,
        )
        value_grad = value_grad + last_weight[:, :, None] * jnp.einsum(
            "sjf,sfd->sjd", key_head.astype(jnp.float32), next_state, precision=PRECISE
        )
        return (query_grad, key_grad, value_grad)

    query_grads, key_grads, value_grads = lax.map(
        head_backward,
        (
            query_heads,
            key_heads,
            value_heads,
            carried[2],
            carried[3],
            numerator_grad,
            denominator_grad,
            state_next,
            total_next,
        ),
    )
    query_rows = to_rows(query_grads)
    key_rows = to_rows(key_grads)
    query_pre_grad = (
        query_rows[..., :head_size] * cosine + query_rows[..., head_size:] * sine_part
    ) * (query_pre > 0.0).astype(jnp.float32)
    key_pre_grad = (key_rows[..., :head_size] * cosine + key_rows[..., head_size:] * sine_part) * (
        key_pre > 0.0
    ).astype(jnp.float32)
    projected_grad = jnp.concatenate(
        [
            query_pre_grad.reshape(row_total, model_width),
            key_pre_grad.reshape(row_total, model_width),
            to_rows(value_grads).reshape(row_total, model_width),
        ],
        axis=1,
    ).astype(jnp.bfloat16)
    in_weight_grad = left_product(flat_tokens, projected_grad)
    in_bias_grad = jnp.sum(projected_grad.astype(jnp.float32), axis=0)
    tokens_grad = (pre_grad + right_product(projected_grad, back_in)).reshape(
        seq_count, length, model_width
    )
    weight_sums = reduce_weights(in_weight_grad, mix_weight_grad, up_weight_grad, down_weight_grad)
    vector_sums = lax.psum(
        (
            in_bias_grad,
            mix_bias_grad,
            first_gain_grad,
            first_shift_grad,
            up_bias_grad,
            down_bias_grad,
            second_gain_grad,
            second_shift_grad,
        ),
        ("row", "col"),
    )
    return (
        layer_out,
        tokens_grad,
        weight_sums[0],
        vector_sums[0],
        weight_sums[1],
        vector_sums[1],
        vector_sums[2],
        vector_sums[3],
        weight_sums[2],
        vector_sums[4],
        weight_sums[3],
        vector_sums[5],
        vector_sums[6],
        vector_sums[7],
    )


def solution(mesh):
    return jax.shard_map(
        per_device,
        mesh=mesh,
        in_specs=(
            P("row", "col", None),
            P("row", "col"),
            P("row", "col"),
            P(),
            P("row", "col"),
            P(),
            P(),
            P(),
            P("row", "col"),
            P(),
            P("row", "col"),
            P(),
            P(),
            P(),
            P("row", "col", None),
        ),
        out_specs=(
            P("row", "col", None),
            P("row", "col", None),
            P("row", "col"),
            P(),
            P("row", "col"),
            P(),
            P(),
            P(),
            P("row", "col"),
            P(),
            P("row", "col"),
            P(),
            P(),
            P(),
        ),
        check_vma=False,
    )
```

profile of v0, /device:TPU:0, one launch (start us, length us, event | category | flops | bytes accessed | tf_op | source)
XLA Modules:
  0.0 1111.4 jit_solution(10756266184303958571)
XLA Ops:
  7.3 8.8 all-gather.11
  22.6 4.5 all-reduce.8
  29.7 53.4 %all-gather.19.cloned.1.call-done = bf16[768,2304]{1,0:T(8,128)(2,1)} async-done(((bf16[96,2304]{1,0:T(8,128)(2,1)}), bf16[768,2304]{1,0:T(8,128)(2,1)}) %all-gather.19.cloned.1.call-update) | async-done | bytes 3538960 | tf_op jit(solution)/shard_map/all_gather | solution.py:118
  83.1 5.8 convolution_add_fusion.4
  89.0 3.5 slice_maximum_fusion
  98.1 3.8 max.32
  104.3 3.7 max.34
  108.1 2.7 copy.118
  110.8 3.8 reshape_reshape.11
  114.6 6.5 multiply_convert_fusion.4
  121.2 7.5 convert_reduce_fusion.2
  131.0 5.6 all_gather.96
  137.5 13.1 %all_gather.98 = bf16[96,3072]{1,0:T(8,128)(2,1)} all-gather(bf16[96,768]{1,0:T(8,128)(2,1)} %param.33), channel_id=1, replica_groups=mesh['row'=8,'col'=4] {'col'}, dimensions={1}, use_global_device_ids=true | all-gather | bytes 737280 | tf_op jit(solution)/shard_map/all_gather | solution.py:114
  150.6 12.1 %all_gather.100 = bf16[384,768]{0,1:T(8,128)(2,1)} all-gather(bf16[384,192]{0,1:T(8,128)(2,1)} %param.35), channel_id=1, replica_groups=mesh['row'=8,'col'=4] {'col'}, dimensions={1}, use_global_device_ids=true | all-gather | bytes 737280 | tf_op jit(solution)/shard_map/all_gather | solution.py:115
  164.0 7.0 all-reduce.10
  172.4 2.9 copy.196
  176.7 5.2 all-gather.4
  181.9 5.6 copy.124
  187.5 8.5 broadcast_multiply_fusion
  196.0 5.6 copy.123
  201.7 12.8 %while.89 = (s32[]{:T(128)}, f32[2]{0:T(128)S(1)}, f32[12,2,128,64]{3,2,1,0:T(8,128)}, f32[12,2,128]{2,1,0:T(2,128)S(1)}, s32[]{:T(128)}, /*index=5*/f32[4,2]{1,...) while((s32[]{:T(128)}, f32[2]{0:T(128)S(1)}, ...), condition=%wide.region_7.8_spmd.clone.clone, body=%wide.region_6.7_spmd.clone.sunk.clone | while | flops 798744 | bytes 5542076 | solution.py:29
  206.7 2.9 fusion.252
  211.4 2.9 fusion.252
  216.3 85.5 %while.87 = (s32[]{:T(128)}, f32[12,2,512,64]{2,3,1,0:T(8,128)}, f32[12,2,512]{2,1,0:T(2,128)}, bf16[12,2,512,128]{3,2,1,0:T(8,128)(2,1)}, bf16[12,2,512,128]{3,...) while((s32[]{:T(128)}, f32[12,2,512,64]{2,3,1,0:T(8,128)}, ...), condition=%wide.region_10.11_spmd.clone.clone, body=%wide.region_8.10_spmd.clone.sunk.clone | while | flops 307957760 | bytes 4725873 | solution.py:276
  307.5 3.9 fusion.148
  312.0 36.4 %multiply_convert_fusion = (bf16[1024,3072]{1,0:T(8,128)(2,1)}, f32[1024,3072]{1,0:T(8,128)}, f32[1024,3072]{1,0:T(8,128)}) fusion(f32[3072]{0:T(1024)S(1)} %convert_element_type.280, bf16[768,3072]{1,0:T(8,128)(2,1)} %all-gather.23.cloned.1.call-done, f32[1024,768]{1,0:T(8,128)S(1)} %get-tuple-element.1175, f32[768]{0:T(1024)S(1)} %convert_element_type.278, ...), kind=kOutput, calls=%fused_computation.145 | convolution fusion | flops 5043388416 | bytes 39348224 | tf_op jit(solution)/shard_map/dot_general | solution.py:288
  348.3 21.2 %all-gather.25.cloned.1.call-done = bf16[3072,768]{0,1:T(8,128)(2,1)} async-done(((bf16[384,768]{0,1:T(8,128)(2,1)}), bf16[3072,768]{0,1:T(8,128)(2,1)}) %all-gather.25.cloned.1.call-update) | async-done | bytes 4718608 | tf_op jit(solution)/shard_map/all_gather | solution.py:121
  369.5 8.9 fusion.149
  381.9 2.7 fusion.142
  385.6 17.2 %convert_reduce_fusion = (f32[3072]{0:T(1024)S(1)}, bf16[1024,3072]{1,0:T(8,128)(2,1)}) fusion(f32[1024,3072]{1,0:T(8,128)} %get-tuple-element.1141, bf16[1024,768]{1,0:T(8,128)(2,1)S(1)} %get-tuple-element.1129, bf16[3072,768]{0,1:T(8,128)(2,1)} %all-gather.25.cloned.1.call-done, f32[1024,3072]{1,0:T(8,128)} %get-tuple-element.1176, ...), kind=kOutput, calls=%fused_computation.143 | convolution fusion | flops 4885312512 | bytes 37773312 | tf_op jit(solution)/shard_map/dot_general | solution.py:74
  402.9 9.8 multiply_reduce_fusion
  417.3 3.0 fusion.150
  420.3 5.7 reshape_reshape.12
  426.1 4.5 fusion.114
  434.5 5.9 all-reduce.11
  441.9 3.7 slice_compare_fusion.1
  451.8 2.5 fusion.121
  454.3 5.6 all-gather.6
  462.7 6.3 while.86
  470.0 162.6 %while.90 = (s32[]{:T(128)}, f32[12,2,512,128]{3,2,1,0:T(8,128)}, f32[12,2,512,128]{3,2,1,0:T(8,128)}, bf16[12,2,512,64]{2,3,1,0:T(8,128)(2,1)}, bf16[12,2,512,6...) while((s32[]{:T(128)}, f32[12,2,512,128]{3,2,1,0:T(8,128)}, ...), condition=%wide.region_23.24_spmd.clone.clone.clone, body=%wide.region_22.23_spmd.clone.clone.sunk.clone | while | flops 847249408 | bytes 9824421 | solution.py:399
  481.1 2.5 fusion.275
  494.6 2.5 fusion.275
  535.3 2.5 fusion.275
  632.7 10.9 fusion.146
  643.6 4.4 copy.165
  648.0 6.1 copy.166
  654.1 11.0 fusion.147
  665.1 6.2 copy.167
  671.3 6.3 copy.168
  677.6 3.2 copy.144
  681.2 5.0 select_convert_fusion.2
  687.9 8.7 fusion.113
  698.0 10.0 convolution_convert_fusion
  709.9 10.1 convolution_convert_fusion.1
  722.0 13.4 %reduce-scatter.15.cloned.1.call-done = bf16[768,576]{0,1:T(8,128)(2,1)} async-done(((bf16[768,2304]{0,1:T(8,128)(2,1)}), bf16[768,576]{0,1:T(8,128)(2,1)}) %reduce-scatter.15.cloned.1.call-update) | async-done | bytes 884752 | tf_op jit(solution)/shard_map/reduce_scatter | solution.py:128
  737.7 48.2 %reduce-scatter.23.cloned.1.call-done = bf16[3072,192]{0,1:T(8,128)(2,1)} async-done(((bf16[3072,768]{0,1:T(8,128)(2,1)}), bf16[3072,192]{0,1:T(8,128)(2,1)}) %reduce-scatter.23.cloned.1.call-update) | async-done | bytes 1179664 | tf_op jit(solution)/shard_map/reduce_scatter | solution.py:137
  788.5 47.6 %reduce-scatter.19.cloned.1.call-done = bf16[768,768]{1,0:T(8,128)(2,1)} async-done(((bf16[768,3072]{1,0:T(8,128)(2,1)}), bf16[768,768]{1,0:T(8,128)(2,1)}) %reduce-scatter.19.cloned.1.call-update) | async-done | bytes 1179664 | tf_op jit(solution)/shard_map/reduce_scatter | solution.py:134
  836.5 2.9 convert_reduce_fusion.1
  839.4 40.9 %all-reduce.9 = (f32[2304]{0:T(1024)}, f32[768]{0:T(1024)}, f32[768]{0:T(1024)}, f32[768]{0:T(1024)}, f32[3072]{0:T(1024)}, /*index=5*/f32[768]{0:T(1024)}, f32[768]{0:T(1024)}, f32[768]{0:T(1024)}) all-reduce(f32[2304]{0:T(1024)S(1)} %convert_reduce_fusion.1, ...), channel_id=1, replica_groups=mesh['row'=8,'col'=4] {'row','col'}, use_global_device_ids=true, to_apply=%region_27.28 | all-reduce | flops 9984 | bytes 79872 | tf_op jit(solution)/shard_map/psum | solution.py:435
  880.3 9.3 add_add_fusion.4
  889.5 12.2 %reduce-scatter.27.cloned.1.call-done = bf16[96,192]{1,0:T(8,128)(2,1)} async-done(((bf16[768,192]{1,0:T(8,128)(2,1)}), bf16[96,192]{1,0:T(8,128)(2,1)}) %reduce-scatter.27.cloned.1.call-update) | async-done | bytes 36880
  903.4 64.7 %reduce-scatter.25.cloned.1.call-done = bf16[96,576]{1,0:T(8,128)(2,1)} async-done(((bf16[768,576]{1,0:T(8,128)(2,1)}), bf16[96,576]{1,0:T(8,128)(2,1)}) %reduce-scatter.25.cloned.1.call-update) | async-done | bytes 110608
  970.0 66.1 %reduce-scatter.29.cloned.1.call-done = bf16[384,192]{1,0:T(8,128)(2,1)} async-done(((bf16[3072,192]{1,0:T(8,128)(2,1)}), bf16[384,192]{1,0:T(8,128)(2,1)}) %reduce-scatter.29.cloned.1.call-update) | async-done | bytes 147472
  1037.9 65.0 %reduce-scatter.21.cloned.1.call-done = bf16[96,768]{1,0:T(8,128)(2,1)} async-done(((bf16[768,768]{1,0:T(8,128)(2,1)}), bf16[96,768]{1,0:T(8,128)(2,1)}) %reduce-scatter.21.cloned.1.call-update) | async-done | bytes 147472 | tf_op jit(solution)/shard_map/reduce_scatter | solution.py:148
  (484 shorter events, 328.3 us)
Async XLA Ops:
  7.2 22.3 %copy-start.33 = (s32[2,512]{1,0:T(2,128)S(1)}, s32[2,512]{1,0:T(2,128)}, u32[]{:S(2)}) copy-start(s32[2,512]{1,0:T(2,128)} %param.26) | copy-start | bytes 12292
  7.2 22.5 %copy-start.42 = (bf16[2304]{0:T(1024)(128)(2,1)S(1)}, bf16[2304]{0:T(1024)(128)(2,1)}, u32[]{:S(2)}) copy-start(bf16[2304]{0:T(1024)(128)(2,1)} %param.28) | copy-start | bytes 13828
  7.2 75.9 %copy-start.52 = (bf16[2,512,768]{2,1,0:T(8,128)(2,1)S(1)}, bf16[2,512,768]{2,1,0:T(8,128)(2,1)}, u32[]{:S(2)}) copy-start(bf16[2,512,768]{2,1,0:T(8,128)(2,1)} %param.25) | copy-start | bytes 4718596
  7.2 75.9 %all-gather.19.cloned.1.call-start = ((), (), s32[]{:S(2)}) async-start(), calls=%async_computation.8 | async-start | bytes 3981312 | tf_op jit(solution)/shard_map/all_gather | solution.py:118
  17.5 184.2 %all-gather.27.cloned.1.call-start = ((), (), s32[]{:S(2)}) async-start(), calls=%async_computation.17 | async-start | bytes 3932160 | tf_op jit(solution)/shard_map/all_gather | solution.py:20
  20.4 6.9 copy-start.50
  29.6 85.0 %copy-start.36 = (f32[2,512]{1,0:T(2,128)}, f32[2,512]{1,0:T(2,128)S(1)}, u32[]{:S(2)}) copy-start(f32[2,512]{1,0:T(2,128)S(1)} %get-tuple-element.1145) | copy-start | bytes 12292
  29.7 84.9 %copy-start.38 = (f32[2,512]{1,0:T(2,128)}, f32[2,512]{1,0:T(2,128)S(1)}, u32[]{:S(2)}) copy-start(f32[2,512]{1,0:T(2,128)S(1)} %sin.11) | copy-start | bytes 12292
  89.0 5.5 copy-start.2
  108.1 6.6 copy-start.8
  121.2 7.5 copy-start.11
  128.6 2.2 copy-start.35
  130.7 41.5 %copy-start.44 = (bf16[768]{0:T(1024)(128)(2,1)S(1)}, bf16[768]{0:T(1024)(128)(2,1)}, u32[]{:S(2)}) copy-start(bf16[768]{0:T(1024)(128)(2,1)} %param.30) | copy-start | bytes 4612
  130.7 41.5 %copy-start.45 = (bf16[768]{0:T(1024)(128)(2,1)S(1)}, bf16[768]{0:T(1024)(128)(2,1)}, u32[]{:S(2)}) copy-start(bf16[768]{0:T(1024)(128)(2,1)} %param.31) | copy-start | bytes 4612
  130.7 41.5 %copy-start.46 = (bf16[768]{0:T(1024)(128)(2,1)S(1)}, bf16[768]{0:T(1024)(128)(2,1)}, u32[]{:S(2)}) copy-start(bf16[768]{0:T(1024)(128)(2,1)} %param.32) | copy-start | bytes 4612
  130.7 41.5 %copy-start.43 = (bf16[3072]{0:T(1024)(128)(2,1)S(1)}, bf16[3072]{0:T(1024)(128)(2,1)}, u32[]{:S(2)}) copy-start(bf16[3072]{0:T(1024)(128)(2,1)} %param.34) | copy-start | bytes 18436
  130.8 41.5 %copy-start.47 = (bf16[768]{0:T(1024)(128)(2,1)S(1)}, bf16[768]{0:T(1024)(128)(2,1)}, u32[]{:S(2)}) copy-start(bf16[768]{0:T(1024)(128)(2,1)} %param.36) | copy-start | bytes 4612
  130.8 41.5 %copy-start.48 = (bf16[768]{0:T(1024)(128)(2,1)S(1)}, bf16[768]{0:T(1024)(128)(2,1)}, u32[]{:S(2)}) copy-start(bf16[768]{0:T(1024)(128)(2,1)} %param.37) | copy-start | bytes 4612
  130.8 41.6 %copy-start.49 = (bf16[768]{0:T(1024)(128)(2,1)S(1)}, bf16[768]{0:T(1024)(128)(2,1)}, u32[]{:S(2)}) copy-start(bf16[768]{0:T(1024)(128)(2,1)} %param.38) | copy-start | bytes 4612
  130.8 176.7 %all-gather.21.cloned.1.call-start = ((), (), s32[]{:S(2)}) async-start(), calls=%async_computation.9 | async-start | bytes 1327104 | tf_op jit(solution)/shard_map/all_gather | solution.py:119
  137.4 174.5 %all-gather.23.cloned.1.call-start = ((), (), s32[]{:S(2)}) async-start(), calls=%async_computation.10 | async-start | bytes 5308416 | tf_op jit(solution)/shard_map/all_gather | solution.py:120
  150.6 218.9 %all-gather.25.cloned.1.call-start = ((), (), s32[]{:S(2)}) async-start(), calls=%async_computation.11 | async-start | bytes 5308416 | tf_op jit(solution)/shard_map/all_gather | solution.py:121
  162.7 299.8 %all-gather.29.cloned.1.call-start = ((), (), s32[]{:S(2)}) async-start(), calls=%async_computation.18 | async-start | bytes 1966080 | tf_op jit(solution)/shard_map/all_gather | solution.py:37
  163.5 24.0 %copy-start.27 = (pred[512,512]{1,0:T(8,128)(4,1)}, pred[512,512]{1,0:T(8,128)(4,1)S(1)}, u32[]{:S(2)}) copy-start(pred[512,512]{1,0:T(8,128)(4,1)S(1)} %iota_compare_fusion) | copy-start | bytes 786436
  201.7 14.6 %copy-start.31 = (pred[512,512]{0,1:T(8,128)(4,1)S(1)}, pred[512,512]{0,1:T(8,128)(4,1)}, u32[]{:S(2)}) copy-start(pred[512,512]{0,1:T(8,128)(4,1)} %copy.126) | copy-start | bytes 786436
  301.9 4.0 copy-start.19
  301.9 4.1 copy-start.25
  301.9 4.1 copy-start.30
  311.4 101.3 %copy-start.5 = (f32[1024,768]{1,0:T(8,128)}, f32[1024,768]{1,0:T(8,128)S(1)}, u32[]{:S(2)}) copy-start(f32[1024,768]{1,0:T(8,128)S(1)} %get-tuple-element.1175) | copy-start | bytes 9437188
  378.4 1.9 copy-start
  385.6 17.3 %copy-start.21 = (bf16[1024,768]{1,0:T(8,128)(2,1)}, bf16[1024,768]{1,0:T(8,128)(2,1)S(1)}, u32[]{:S(2)}) copy-start(bf16[1024,768]{1,0:T(8,128)(2,1)S(1)} %get-tuple-element.1129) | copy-start | bytes 4718596
  414.2 1.7 copy-start.3
  414.2 3.1 copy-start.54
  420.3 5.8 copy-start.32
  420.3 5.8 copy-start.7
  426.1 5.7 copy-start.17
  431.8 2.1 copy-start.34
  431.8 8.7 copy-start.39
  431.8 8.7 copy-start.37
  433.8 286.3 %reduce-scatter.17.cloned.1.call-start = ((), (), s32[]{:S(2)}) async-start(), calls=%async_computation.13 | async-start | bytes 1474560 | tf_op jit(solution)/shard_map/reduce_scatter | solution.py:131
  445.6 3.7 copy-start.14
  449.3 2.5 copy-start.18
  450.8 9.2 copy-start.20
  450.8 9.2 copy-start.24
  462.4 273.0 %reduce-scatter.15.cloned.1.call-start = ((), (), s32[]{:S(2)}) async-start(), calls=%async_computation.12 | async-start | bytes 4423680 | tf_op jit(solution)/shard_map/reduce_scatter | solution.py:128
  462.7 6.4 copy-start.51
  677.6 3.6 copy-start.9
  677.6 3.6 copy-start.10
  681.2 5.1 copy-start.12
  681.2 6.7 copy-start.53
  686.3 1.2 copy-start.15
  686.3 1.6 copy-start.16
  696.6 1.4 copy-start.22
  696.6 89.3 %reduce-scatter.23.cloned.1.call-start = ((), (), s32[]{:S(2)}) async-start(), calls=%async_computation.16 | async-start | bytes 5898240 | tf_op jit(solution)/shard_map/reduce_scatter | solution.py:137
  708.0 1.9 copy-start.6
  708.0 128.1 %reduce-scatter.19.cloned.1.call-start = ((), (), s32[]{:S(2)}) async-start(), calls=%async_computation.14 | async-start | bytes 5898240 | tf_op jit(solution)/shard_map/reduce_scatter | solution.py:134
  720.0 181.7 %reduce-scatter.27.cloned.1.call-start = ((), (), s32[]{:S(2)}) async-start(), calls=%async_computation.20 | async-start | bytes 442368
  722.0 246.1 %reduce-scatter.25.cloned.1.call-start = ((), (), s32[]{:S(2)}) async-start(), calls=%async_computation.19 | async-start | bytes 1105920
  737.6 98.5 %copy-start.1 = (f32[2,512,768]{2,1,0:T(8,128)S(1)}, f32[2,512,768]{2,1,0:T(8,128)}, u32[]{:S(2)}) copy-start(f32[2,512,768]{2,1,0:T(8,128)} %param.39) | copy-start | bytes 9437188
  737.7 298.4 %reduce-scatter.29.cloned.1.call-start = ((), (), s32[]{:S(2)}) async-start(), calls=%async_computation.21 | async-start | bytes 1769472
  788.5 314.5 %reduce-scatter.21.cloned.1.call-start = ((), (), s32[]{:S(2)}) async-start(), calls=%async_computation.15 | async-start | bytes 1327104 | tf_op jit(solution)/shard_map/reduce_scatter | solution.py:148
  836.4 2.9 copy-start.40
  836.5 2.9 copy-start.41
  836.5 43.8 %copy-start.4 = (f32[1024,768]{1,0:T(8,128)S(1)}, f32[1024,768]{1,0:T(8,128)}, u32[]{:S(2)}) copy-start(f32[1024,768]{1,0:T(8,128)} %copy-done.3) | copy-start | bytes 9437188
  (5 other events, 5.0 us)
Sparse Core Ops, SparseCore 0:
  17.6 65.4 all-gather.18
  130.9 33.6 all-gather.26
  167.3 41.0 all-gather.20
  210.5 78.0 all-gather.22
  290.4 78.9 all-gather.24
  433.9 17.7 all-gather.28
  462.6 24.0 reduce-scatter.16
  696.7 38.6 reduce-scatter.14
  738.0 47.9 reduce-scatter.22
  788.3 47.7 reduce-scatter.18
  839.4 62.2 reduce-scatter.26
  904.9 63.1 reduce-scatter.24
  971.5 64.5 reduce-scatter.28
  1039.4 63.5 reduce-scatter.20
where the time goes:
time: 1130 us; the launch traced here: 1110 us
  waiting for transfers between devices  392 us (35%)
  matrix products  364 us (32%)
  local copies, waits for them, and re-layouts  151 us (13%)
  blocking collectives  109 us (10%)
  other arithmetic  77.7 us (7%)
  between operations  15.8 us (1%)
    unnamed x17, waiting for transfers between devices  143 us
    unnamed x148, local copies, waits for them, and re-layouts  69.2 us
    reduce_scatter x1, waiting for transfers between devices, reduce_weights(): lax.psum_scatter(partial_value[2].astype(jnp.bfloat16), 'row', scatter_di...  65 us
    all_gather x1, waiting for transfers between devices, fetch_weights(): lax.all_gather(partial_value[0], 'row', axis=0, tiled=True)  53.4 us
    reduce_scatter x1, waiting for transfers between devices, reduce_weights(): lax.psum_scatter(down_grad.astype(jnp.bfloat16), 'col', scatter_dimension...  48.2 us
    reduce_scatter x1, waiting for transfers between devices, reduce_weights(): lax.psum_scatter(up_grad.astype(jnp.bfloat16), 'col', scatter_dimension=1...  47.6 us
    psum x1, blocking collectives, per_device(): lax.psum((in_bias_grad, mix_bias_grad, first_gain_grad, first_shift_grad,...  40.9 us
    dot_general x4, matrix products, right_product(): lax.dot_general(first, second, (((1,), (1,)), ((), ())), preferred_elemen...  39.3 us
  transfers between devices with their start and end apart: 14, of which 9 were waited for; matrix products, arithmetic and copies ran while one was open for 42% of the time, Pallas kernels for 0%

commit v1 on v0

v1 whole, which is shorter than its diff:
```python
import functools
import math

import jax
import jax.numpy as jnp
from jax import lax
from jax.experimental import pallas as pl
from jax.experimental.pallas import tpu as pltpu
from jax.sharding import PartitionSpec as P

HEADS = 12
HEAD_DIM = 64
DOC_MAX = 2000
EPSILON = 1e-05
FLOOR = 4.0
OMEGA = math.pi / (2.0 * DOC_MAX)
MESH = pl.DeviceIdType.MESH
F32 = jnp.float32
BF16 = jnp.bfloat16
VMEM_LIMIT = 67_043_328

NN = (((1,), (0,)), ((), ()))
NT = (((1,), (1,)), ((), ()))
TN = (((0,), (0,)), ((), ()))


def dot(first, second, dims=NN):
    return lax.dot_general(first, second, dims, preferred_element_type=F32)


class Layout:
    def __init__(self, rows, cols):
        self.R, self.C = rows, cols
        self.Z = 4 if rows % 4 == 0 else rows
        self.Y = rows // self.Z
        self.K = 2
        self.X = cols // 2
        self.hops = (self.Z - 1) + (self.Y - 1) + (self.X - 1) + 1


class Place:
    def __init__(self, lay):
        self.lay = lay
        self.r = lax.axis_index("row")
        self.c = lax.axis_index("col")
        self.z, self.y = self.r // lay.Y, self.r % lay.Y
        self.x, self.k = self.c // 2, self.c % 2

    def at(self, z=None, y=None, x=None, k=None):
        z = self.z if z is None else z
        y = self.y if y is None else y
        x = self.x if x is None else x
        k = self.k if k is None else k
        return {"row": z * self.lay.Y + y, "col": x * 2 + k}

    def zs(self):
        return [lax.rem(self.z + d, self.lay.Z) for d in range(1, self.lay.Z)]

    def ys(self):
        return [lax.rem(self.y + d, self.lay.Y) for d in range(1, self.lay.Y)]

    def xs(self):
        return [lax.rem(self.x + d, self.lay.X) for d in range(1, self.lay.X)]

    def ring(self, step):
        return {"row": self.r, "col": lax.rem(self.c + step + self.lay.C, self.lay.C)}

    def barrier(self):
        peers = [self.at(z=z) for z in self.zs()] + [self.at(y=y) for y in self.ys()]
        peers += [self.at(x=x) for x in self.xs()] + [self.at(k=1 - self.k)]
        peers += [self.ring(1), self.ring(-1)]
        sem = pltpu.get_barrier_semaphore()
        for peer in peers:
            pl.semaphore_signal(sem, inc=1, device_id=peer, device_id_type=MESH)
        pl.semaphore_wait(sem, len(peers))


def remote(src, dst, send, recv, device):
    return pltpu.make_async_remote_copy(
        src_ref=src, dst_ref=dst, send_sem=send, recv_sem=recv, device_id=device, device_id_type=MESH
    )


class Gather:
    def __init__(self, place, shard, whole, r0, n, y_first, send, recv, base):
        self.p, self.shard, self.whole = place, shard, whole
        self.rows = pl.ds(r0, n)
        self.y_first = y_first
        self.send, self.recv, self.base = send, recv, base

    def stage(self, number):
        p, g, rows, lay = self.p, self.whole, self.rows, self.p.lay
        first, copies = self.base, []
        if number == 0:
            for z in p.zs():
                copies.append((self.shard.at[rows], g.at[p.x, p.k, p.z, p.y, rows], p.at(z=z)))
        else:
            first += lay.Z - 1
            along_y = (number == 1) == self.y_first
            if number == 3:
                part = g.at[:, p.k, :, :, rows]
                copies.append((part, part, p.at(k=1 - p.k)))
                first += lay.Y - 1 + lay.X - 1
            else:
                if number == 2:
                    first += (lay.Y - 1) if self.y_first else (lay.X - 1)
                    part = g.at[:, p.k, :, p.y, rows] if along_y else g.at[p.x, p.k, :, :, rows]
                else:
                    part = g.at[p.x, p.k, :, p.y, rows]
                for peer in [p.at(y=y) for y in p.ys()] if along_y else [p.at(x=x) for x in p.xs()]:
                    copies.append((part, part, peer))
        return [
            remote(src, dst, self.send.at[first + i], self.recv.at[first + i], device)
            for i, (src, dst, device) in enumerate(copies)
        ]

    def start(self, number):
        for copy in self.stage(number):
            copy.start()

    def arrive(self, number):
        for copy in self.stage(number):
            copy.wait_recv()

    def advance(self, number):
        self.arrive(number - 1)
        self.start(number)

    def sent(self):
        for number in range(4):
            for copy in self.stage(number):
                copy.wait_send()


def pieces(rows, count):
    tiles, many = rows // 16, 2 * count
    many = min(many, tiles)
    cuts = [(tiles * i + many - 1) // many for i in range(many + 1)]
    return [(cuts[i] * 16, (cuts[i + 1] - cuts[i]) * 16, i % 2 == 1) for i in range(many)]


def lane_half(head):
    lane = lax.broadcasted_iota(jnp.int32, (1, 128), 1)
    return ((lane < 64) if head == 0 else (lane >= 64)).astype(F32)


def same_head():
    row = lax.broadcasted_iota(jnp.int32, (128, 128), 0)
    lane = lax.broadcasted_iota(jnp.int32, (128, 128), 1)
    return ((row < 64) == (lane < 64)).astype(F32)


def seq_masks(ids_ref, prev_ref, seq, length, has_prev):
    row = ids_ref[seq : seq + 1, :].astype(F32)
    column = jnp.transpose(jnp.broadcast_to(row, (128, length)))
    lane = lax.broadcasted_iota(jnp.int32, (1, length), 1)
    first = jnp.sum(jnp.where(lane == 0, row, 0.0), axis=1, keepdims=True)
    last = jnp.sum(jnp.where(lane == length - 1, row, 0.0), axis=1, keepdims=True)
    before = prev_ref[seq : seq + 1, :].astype(F32)
    before = jnp.sum(jnp.where(lane == length - 1, before, 0.0), axis=1, keepdims=True)
    before = jnp.where(has_prev, before, -1.0)
    carry = (column == before).astype(F32)
    last_mask = (column == last).astype(F32)
    passes = ((first == last) & (first == before)).astype(F32)
    return row, column, carry, last_mask, passes


def angle_tables(length):
    column = lax.broadcasted_iota(jnp.int32, (length, 128), 0).astype(F32) * OMEGA
    row = lax.broadcasted_iota(jnp.int32, (1, length), 1).astype(F32) * OMEGA
    return jnp.cos(column), jnp.sin(column), jnp.cos(row), jnp.sin(row)


def edge_angles(cosine, sine, length):
    turn_c, turn_s = math.cos(OMEGA * length), math.sin(OMEGA * length)
    return cosine * turn_c + sine * turn_s, sine * turn_c - cosine * turn_s


def unpack_state(block):
    low, high = lane_half(0), lane_half(1)
    out = []
    for half in (0, 1):
        part = block[0:64, half * 128 : half * 128 + 128].astype(F32)
        out.append(jnp.concatenate([part * low, part * high], axis=0))
    return out


def pack_state(square):
    square = square * same_head()
    return square[0:64] + square[64:128]


def unslot(whole, flat, lay, a, b, transposed):
    for c in range(lay.C):
        if transposed:
            for r in range(lay.R):
                flat[c * a : (c + 1) * a, r * b : (r + 1) * b] = whole[
                    c // 2, c % 2, r // lay.Y, r % lay.Y
                ]
        else:
            for z in range(lay.Z):
                for y in range(lay.Y):
                    r = z * lay.Y + y
                    flat[r * a : (r + 1) * a, c * b : (c + 1) * b] = whole[c // 2, c % 2, z, y]


def forward_kernel(
    lay, seqs, length, cuts,
    tokens, ids, bias, in_s, mix_s, up_s, down_s,
    q_out, k_out, v_out, att, den, carry, prev, full_in, g_mix, g_up, g_down,
    g_in, mask, tab, out_state, flags,
    send, recv, misc_send, misc_recv, local,
):
    p = Place(lay)
    pairs = q_out.shape[1] // 128
    width = q_out.shape[1]
    total = seqs * pairs
    p.barrier()
    flows = []
    base = 0
    groups = []
    for shard, whole, parts in zip(
        (in_s, mix_s, up_s, down_s), (g_in, g_mix, g_up, g_down), cuts, strict=True
    ):
        group = []
        for r0, n, y_first in parts:
            group.append(Gather(p, shard, whole, r0, n, y_first, send, recv, base))
            base += lay.hops
        groups.append(group)
        flows += group
    own = [
        pltpu.make_async_copy(shard, whole.at[p.x, p.k, p.z, p.y], local.at[i])
        for i, (shard, whole) in enumerate(
            zip((in_s, mix_s, up_s, down_s), (g_in, g_mix, g_up, g_down), strict=True)
        )
    ]
    for copy in own:
        copy.start()
    ring_ids = remote(ids, prev, misc_send.at[0], misc_recv.at[0], p.ring(1))
    ring_ids.start()
    for flow in flows:
        flow.start(0)
    for copy in own:
        copy.wait()
    for flow in groups[0]:
        flow.advance(1)

    cos_a, sin_a, cos_r, sin_r = angle_tables(length)
    cos_e, sin_e = edge_angles(cos_a, sin_a, length)
    ring_ids.wait_recv()
    for s in range(seqs):
        row, column, carried, last_mask, passes = seq_masks(ids, prev, s, length, p.c > 0)
        at_i = lax.broadcasted_iota(jnp.int32, (length, length), 0)
        at_j = lax.broadcasted_iota(jnp.int32, (length, length), 1)
        allowed = (column[:, 0:1] == row) & (at_j <= at_i)
        mask[s] = jnp.where(allowed, cos_a[:, 0:1] * cos_r + sin_a[:, 0:1] * sin_r, 0.0)
        tab[s, 0] = cos_a * carried
        tab[s, 1] = sin_a * carried
        tab[s, 2] = cos_e * last_mask
        tab[s, 3] = sin_e * last_mask
        flags[s] = jnp.broadcast_to(passes, (8, 256))

    for number in (2, 3):
        for flow in groups[0]:
            flow.advance(number)
    for flow in groups[0]:
        flow.arrive(3)
    unslot(g_in, full_in, lay, in_s.shape[0], in_s.shape[1], False)

    blocks = width // 256
    half = tokens.shape[0] // 2

    def project(target, start, relu):
        def column_block(j, _):
            lanes = pl.ds(pl.multiple_of(j * 256, 256), 256)
            source = pl.ds(pl.multiple_of(start + j * 256, 256), 256)
            for m in range(2):
                out = dot(tokens[m * half : (m + 1) * half, :], full_in[:, source]) + bias[:, source]
                if relu:
                    out = jnp.maximum(out, 0.0)
                target[m * half : (m + 1) * half, lanes] = out.astype(BF16)
            return 0

        lax.fori_loop(0, blocks, column_block, 0)

    project(q_out, 0, True)
    project(k_out, width, True)
    project(v_out, 2 * width, False)

    def where(it):
        s, pair = it // pairs, it % pairs
        return s, pl.ds(pl.multiple_of(s * length, length), length), pl.ds(pl.multiple_of(pair * 128, 128), 128)

    def local_state(it, _):
        s, rows, lanes = where(it)
        keys, values = k_out[rows, lanes], v_out[rows, lanes].astype(F32)
        scaled = jnp.concatenate([values * tab[s, 2], values * tab[s, 3]], axis=1).astype(BF16)
        state = dot(keys, scaled, TN)
        wide = keys.astype(F32)
        for part in (0, 1):
            packed = pack_state(state[:, part * 128 : part * 128 + 128])
            out_state[it, 0:64, part * 128 : part * 128 + 128] = packed.astype(BF16)
            total_row = jnp.sum(wide * tab[s, 2 + part], axis=0, keepdims=True)
            out_state[it, 64:80, part * 128 : part * 128 + 128] = jnp.broadcast_to(total_row, (16, 128)).astype(BF16)
        return 0

    lax.fori_loop(0, total, local_state, 0)

    def chain_copy():
        return remote(out_state, carry, misc_send.at[1], misc_recv.at[1], p.ring(1))

    turn_c, turn_s = math.cos(OMEGA * length), math.sin(OMEGA * length)

    def hand_on():
        def one(it, _):
            came = carry[it].astype(F32)
            came_c, came_s = came[:, 0:128], came[:, 128:256]
            turned = jnp.concatenate(
                [came_c * turn_c + came_s * turn_s, came_s * turn_c - came_c * turn_s], axis=1
            )
            state = out_state[it].astype(F32) + flags[it // pairs, 0:1, :] * turned
            out_state[it] = state.astype(BF16)
            return 0

        lax.fori_loop(0, total, one, 0)

    def chain_step():
        @pl.when(p.c == 0)
        def _():
            carry[...] = jnp.zeros_like(carry)

        @pl.when(p.c > 0)
        def _():
            chain_copy().wait_recv()
            hand_on()

        @pl.when(p.c < lay.C - 1)
        def _():
            chain_copy().start()

    def fine(number):
        return [functools.partial(f.advance, number) for f in groups[1]], [
            functools.partial(f.advance, number) for f in groups[2]
        ], [functools.partial(f.advance, number) for f in groups[3]]

    m1, u1, d1 = fine(1)
    m2, u2, d2 = fine(2)
    m3, u3, d3 = fine(3)
    thunks = m1 + u1 + m2 + m3 + d1 + u2 + d2 + u3 + d3
    step_block = 256 if length % 256 == 0 else length

    def local_attention(it, _):
        @pl.when(it == (p.c * total) // lay.C)
        def _():
            chain_step()

        for n, thunk in enumerate(thunks):

            @pl.when(it == (n * total) // len(thunks))
            def _(thunk=thunk):
                thunk()

        s, rows, lanes = where(it)
        low, high = lane_half(0), lane_half(1)
        queries, keys, values = q_out[rows, lanes], k_out[rows, lanes], v_out[rows, lanes]
        for b in range(length // step_block):
            lo, reach = b * step_block, (b + 1) * step_block
            q = queries[lo:reach]
            numer = jnp.zeros((step_block, 128), F32)
            denom = jnp.zeros((step_block, 128), F32)
            for side in (low, high):
                only = side.astype(BF16)
                scores = dot(q, keys[:reach] * only, NT) * mask[s, lo:reach, 0:reach]
                numer = numer + dot(scores.astype(BF16), values[:reach] * only)
                denom = denom + jnp.sum(scores, axis=1, keepdims=True) * side
            here = pl.ds(pl.multiple_of(s * length + lo, step_block), step_block)
            att[here, lanes] = numer
            den[here, lanes] = denom
        return 0

    lax.fori_loop(0, total, local_attention, 0)

    square = same_head()

    def finish(it, _):
        s, rows, lanes = where(it)
        state_c, state_s = unpack_state(carry[it])
        totals = []
        for part in (0, 1):
            line = carry[it, 64:80, part * 128 : part * 128 + 128].astype(F32)[0:1]
            totals.append(jnp.transpose(jnp.broadcast_to(line, (128, 128))) * square)
        wide = jnp.concatenate([state_c, state_s, totals[0], totals[1]], axis=1).astype(BF16)
        reach = dot(q_out[rows, lanes], wide)
        c_i, s_i = tab[s, 0], tab[s, 1]
        numer = att[rows, lanes] + c_i * reach[:, 0:128] + s_i * reach[:, 128:256]
        denom = den[rows, lanes] + c_i * reach[:, 256:384] + s_i * reach[:, 384:512]
        den[rows, lanes] = denom
        att[rows, lanes] = numer / jnp.maximum(denom, FLOOR)
        return 0

    lax.fori_loop(0, total, finish, 0)

    for flow in flows[len(groups[0]) :]:
        flow.arrive(3)
    for flow in flows:
        flow.sent()
    ring_ids.wait_send()

    @pl.when(p.c < lay.C - 1)
    def _():
        chain_copy().wait_send()


def forward(lay, tokens, ids, bias, shards):
    seqs, length = ids.shape
    rows, width = tokens.shape
    total = seqs * (width // 128)
    cuts = [pieces(s.shape[0], n) for s, n in zip(shards, (3, 1, 1, 1), strict=True)]
    cuts = tuple(cuts)
    flows = sum(len(c) for c in cuts)
    vmem, anyspace = pl.BlockSpec(memory_space=pltpu.VMEM), pl.BlockSpec(memory_space=pl.ANY)
    slots = [(lay.X, 2, lay.Z, lay.Y) + s.shape for s in shards]
    shape = jax.ShapeDtypeStruct
    outs = (
        [shape((rows, width), BF16)] * 3
        + [shape((rows, width), F32)] * 2
        + [shape((total, 80, 256), BF16), shape(ids.shape, jnp.int32), shape((width, 3 * width), BF16)]
        + [shape(s, BF16) for s in slots[1:]]
    )
    return pl.pallas_call(
        functools.partial(forward_kernel, lay, seqs, length, cuts),
        out_shape=outs,
        in_specs=[vmem] * 7,
        out_specs=[vmem] * 8 + [anyspace] * 3,
        scratch_shapes=[
            pltpu.VMEM(slots[0], BF16),
            pltpu.VMEM((seqs, length, length), F32),
            pltpu.VMEM((seqs, 4, length, 128), F32),
                pltpu.VMEM((total, 80, 256), BF16),
            pltpu.VMEM((seqs, 8, 256), F32),
                pltpu.SemaphoreType.DMA((flows * lay.hops,)),
            pltpu.SemaphoreType.DMA((flows * lay.hops,)),
            pltpu.SemaphoreType.DMA((2,)),
            pltpu.SemaphoreType.DMA((2,)),
            pltpu.SemaphoreType.DMA((4,)),
        ],
        compiler_params=pltpu.CompilerParams(
            collective_id=0, has_side_effects=True, vmem_limit_bytes=VMEM_LIMIT
        ),
        name="forward_attention",
    )(tokens, ids, bias, *shards)


def normalize(values):
    center = values - jnp.mean(values, axis=-1, keepdims=True)
    scale = lax.rsqrt(jnp.mean(center * center, axis=-1, keepdims=True) + EPSILON)
    return center * scale, scale


def normalize_grad(grad, unit, scale):
    return (
        grad
        - jnp.mean(grad, axis=-1, keepdims=True)
        - unit * jnp.mean(grad * unit, axis=-1, keepdims=True)
    ) * scale


def rows_sum(values):
    return jnp.sum(values, axis=0, keepdims=True)


def dense_kernel(
    lay, row_blocks, chunk, direct,
    tokens, att, den, cot, mix_b, up_b, down_b, gain1, shift1, gain2, shift2, g_mix, g_up, g_down,
    layer_out, pre_out, given_out, tok_t, d_mix, d_up, d_down, sums,
    w_mix, w_up, w_down, mix_raw, act, up_g, hid_t, down_t, att_t, mix_g, slope, acc, sem,
):
    step = pl.program_id(0)
    block, width = tokens.shape
    ff = act.shape[1]
    chunks = ff // chunk
    mix_a, mix_w = d_mix.shape[-2:]
    up_w = d_up.shape[-1]
    down_a, down_w = d_down.shape[-2:]

    def fetch_mix():
        return [pltpu.make_async_copy(g_mix, mix_raw, sem.at[0])]

    def fetch_up():
        if not direct:
            return [pltpu.make_async_copy(g_up, w_up, sem.at[1])]
        return [
            pltpu.make_async_copy(g_up.at[c // 2, c % 2], w_up.at[:, :, :, pl.ds(c * up_w, up_w)], sem.at[3 + c])
            for c in range(lay.C)
        ]

    def fetch_down():
        if not direct:
            return [pltpu.make_async_copy(g_down, w_down, sem.at[2])]
        return [
            pltpu.make_async_copy(
                g_down.at[c // 2, c % 2, r // lay.Y, r % lay.Y],
                w_down.at[c, :, pl.ds(r * down_w, down_w)],
                sem.at[3 + lay.C + c * lay.R + r],
            )
            for c in range(lay.C)
            for r in range(lay.R)
        ]

    def up_chunk(lanes):
        return w_up[:, :, :, lanes].reshape(width, chunk)

    def down_chunk(lanes):
        return w_down[:, :, lanes].reshape(width, chunk)

    @pl.when(step == 0)
    def _():
        for copy in fetch_mix() + fetch_up() + fetch_down():
            copy.start()
        acc[...] = jnp.zeros_like(acc)
        for copy in fetch_mix():
            copy.wait()
        unslot(mix_raw, w_mix, lay, mix_a, mix_w, False)

    @pl.when(step < row_blocks)
    def _():
        rows = pl.ds(pl.multiple_of(step * block, block), block)
        att_low = att[...].astype(BF16)
        att_t[:, rows] = jnp.transpose(att_low)
        tok_t[...] = jnp.transpose(tokens[...])
        mixed = dot(att_low, w_mix[...]) + mix_b[...]
        unit1, scale1 = normalize(tokens[...].astype(F32) + mixed)
        hidden = unit1 * gain1[...] + shift1[...]
        hidden_low = hidden.astype(BF16)
        hid_t[:, rows] = jnp.transpose(hidden_low)

        @pl.when(step == 0)
        def _():
            for copy in fetch_up() + fetch_down():
                copy.wait()

        def up_down(n, total):
            lanes = pl.ds(pl.multiple_of(n * chunk, chunk), chunk)
            up = dot(hidden_low, up_chunk(lanes)) + up_b[:, lanes]
            cdf = 0.5 + 0.5 * lax.erf(up * math.sqrt(0.5))
            density = jnp.exp(up * up * -0.5) * (1.0 / math.sqrt(2.0 * math.pi))
            slope[:, lanes] = cdf + up * density
            active = (up * cdf).astype(BF16)
            act[rows, lanes] = active
            return total + dot(active, down_chunk(lanes), NT)

        down = lax.fori_loop(0, chunks, up_down, jnp.zeros((block, width), F32)) + down_b[...]
        unit2, scale2 = normalize(hidden + down)
        layer_out[...] = (unit2 * gain2[...] + shift2[...]).astype(BF16)
        given = cot[...]
        acc[3:4, 0:width] += rows_sum(given * unit2)
        acc[3:4, width : 2 * width] += rows_sum(given)
        sum_grad = normalize_grad(given * gain2[...], unit2, scale2)
        down_grad = sum_grad.astype(BF16)
        down_t[:, rows] = jnp.transpose(down_grad)
        acc[2:3, 3 * width : 4 * width] += rows_sum(down_grad.astype(F32))

        def back(n, total):
            lanes = pl.ds(pl.multiple_of(n * chunk, chunk), chunk)
            grad = (dot(down_grad, down_chunk(lanes)) * slope[:, lanes]).astype(BF16)
            up_g[rows, lanes] = grad
            acc[0:1, lanes] += rows_sum(grad.astype(F32))
            return total + dot(grad, up_chunk(lanes), NT)

        hidden_grad = lax.fori_loop(0, chunks, back, sum_grad)
        acc[2:3, width : 2 * width] += rows_sum(hidden_grad * unit1)
        acc[2:3, 2 * width : 3 * width] += rows_sum(hidden_grad)
        pre_grad = normalize_grad(hidden_grad * gain1[...], unit1, scale1)
        pre_out[...] = pre_grad
        mixed_grad = pre_grad.astype(BF16)
        mix_g[rows, :] = mixed_grad
        acc[2:3, 0:width] += rows_sum(mixed_grad.astype(F32))
        att_grad = dot(mixed_grad, w_mix[...], NT)
        denom = den[...]
        inverse = 1.0 / jnp.maximum(denom, FLOOR)
        numer = att_grad * inverse
        weighted = att_grad * att[...]
        upper = weighted.astype(BF16)
        lower = (weighted - upper.astype(F32)).astype(BF16)
        square = same_head().astype(BF16)
        factor = inverse * (denom > FLOOR).astype(F32)
        lane = lax.broadcasted_iota(jnp.int32, (1, 128), 1)
        for t in range(width // 128):
            lanes = slice(t * 128, t * 128 + 128)
            summed = dot(upper[:, lanes], square) + dot(lower[:, lanes], square)
            extra = -summed * factor[:, lanes]
            extra = jnp.concatenate([extra[:, 64:128], extra[:, 0:64]], axis=1)
            extra_hi = extra.astype(BF16).astype(F32)
            for head in (0, 1):
                spare = 64 - 64 * head
                both = (
                    numer[:, lanes] * lane_half(head)
                    + extra_hi * (lane == spare).astype(F32)
                    + (extra - extra_hi) * (lane == spare + 1).astype(F32)
                )
                at = t * 256 + head * 128
                given_out[:, at : at + 128] = both.astype(BF16)

    @pl.when(step >= row_blocks)
    def _():
        n = step - row_blocks
        lanes = pl.ds(pl.multiple_of(n * chunk, chunk), chunk)
        up_part = dot(hid_t[...], up_g[:, lanes]).astype(BF16)
        for i in range(chunk // up_w):
            d_up[i // 2, i % 2] = up_part[:, i * up_w : (i + 1) * up_w].reshape(d_up.shape[2:])
        down_part = dot(down_t[...], act[:, lanes]).astype(BF16)
        for c in range(lay.C):
            for y in range(lay.Y):
                d_down[c // 2, c % 2, 0, y] = down_part[
                    c * down_a : (c + 1) * down_a, y * down_w : (y + 1) * down_w
                ]

    @pl.when(step == row_blocks)
    def _():
        mix_part = dot(att_t[...], mix_g[...]).astype(BF16)
        for c in range(lay.C):
            d_mix[c // 2, c % 2] = mix_part[:, c * mix_w : (c + 1) * mix_w].reshape(d_mix.shape[2:])
        sums[...] = acc[...]


def dense(lay, tokens, att, den, cot, vectors, g_mix, g_up, g_down):
    total, width = tokens.shape
    block = 256 if total % 256 == 0 else total
    row_blocks = total // block
    ff = g_up.shape[-1] * lay.C
    chunk = ff // lay.Z
    up_w, down_w = g_up.shape[-1], g_down.shape[-1]
    direct = up_w % 128 == 0 and down_w % 128 == 0
    slots = [g.shape for g in (g_mix, g_up, g_down)]
    if not direct:
        g_up = g_up.transpose(2, 3, 4, 0, 1, 5).reshape(lay.Z, lay.Y, g_up.shape[4], ff)
        g_down = g_down.transpose(0, 1, 4, 2, 3, 5).reshape(lay.C, g_down.shape[4], ff)
    last = row_blocks - 1
    per = chunk // up_w
    by_row = pl.BlockSpec((block, width), lambda i: (jnp.minimum(i, last), 0))
    fixed = lambda shape: pl.BlockSpec(shape, lambda i: (0,) * len(shape), pipeline_mode=pl.Buffered(1))
    anyspace = pl.BlockSpec(memory_space=pl.ANY)
    later = lambda i: jnp.maximum(i - row_blocks, 0)
    if per == 1:
        up_spec = pl.BlockSpec((1, 1) + slots[1][2:], lambda i: (later(i) // 2, later(i) % 2, 0, 0, 0, 0))
    else:
        up_spec = pl.BlockSpec((per // 2, 2) + slots[1][2:], lambda i: (later(i), 0, 0, 0, 0, 0))
    down_spec = pl.BlockSpec(slots[2][:2] + (1,) + slots[2][3:], lambda i: (0, 0, later(i), 0, 0, 0))
    shape = jax.ShapeDtypeStruct
    return pl.pallas_call(
        functools.partial(dense_kernel, lay, row_blocks, chunk, direct),
        grid=(row_blocks + lay.Z,),
        out_shape=[
            shape((total, width), BF16),
            shape((total, width), F32),
            shape((total, 2 * width), BF16),
            shape((width, total), BF16),
            shape(slots[0], BF16),
            shape(slots[1], BF16),
            shape(slots[2], BF16),
            shape((4, ff), F32),
        ],
        in_specs=[by_row] * 4 + [fixed(v.shape) for v in vectors] + [anyspace] * 3,
        out_specs=[
            by_row,
            by_row,
            pl.BlockSpec((block, 2 * width), lambda i: (jnp.minimum(i, last), 0)),
            pl.BlockSpec((width, block), lambda i: (0, jnp.minimum(i, last))),
            fixed(slots[0]),
            up_spec,
            down_spec,
            fixed((4, ff)),
        ],
        scratch_shapes=[
            pltpu.VMEM((width, width), BF16),
            pltpu.VMEM((lay.Z, lay.Y, slots[1][4], ff), BF16),
            pltpu.VMEM((lay.C, slots[2][4], ff), BF16),
            pltpu.VMEM(slots[0], BF16),
            pltpu.VMEM((total, ff), BF16),
            pltpu.VMEM((total, ff), BF16),
            pltpu.VMEM((width, total), BF16),
            pltpu.VMEM((width, total), BF16),
            pltpu.VMEM((width, total), BF16),
            pltpu.VMEM((total, width), BF16),
            pltpu.VMEM((block, ff), F32),
            pltpu.VMEM((4, ff), F32),
            pltpu.SemaphoreType.DMA((3 + lay.C + lay.C * lay.R,)),
        ],
        compiler_params=pltpu.CompilerParams(vmem_limit_bytes=VMEM_LIMIT),
        name="dense",
    )(tokens, att, den, cot, *vectors, g_mix, g_up, g_down)


class Scatter:
    def __init__(self, place, source, mine, came, second, third, fourth, target, r0, n, y_first, send, recv, base, fetch):
        self.p, self.source, self.mine, self.came = place, source, mine, came
        self.second, self.third, self.fourth, self.target = second, third, fourth, target
        self.rows, self.r0, self.n, self.y_first = pl.ds(r0, n), r0, n, y_first
        self.send, self.recv, self.base, self.fetch = send, recv, base, fetch

    def stage(self, number):
        p, rows, lay, mine = self.p, self.rows, self.p.lay, self.mine
        first, copies = self.base, []
        if number == 0:
            copies.append(
                (self.source.at[:, 1 - p.k, :, :, rows], self.came.at[:, :, :, rows], p.at(k=1 - p.k))
            )
        elif number == 3:
            first += 1 + lay.X - 1 + lay.Y - 1
            for d, z in enumerate(p.zs()):
                copies.append((mine.at[p.x, z, p.y, rows], self.fourth.at[d], p.at(z=z)))
        else:
            along_y = (number == 1) == self.y_first
            landing = self.second if number == 1 else self.third
            first += 1
            if number == 2:
                first += (lay.Y - 1) if self.y_first else (lay.X - 1)
            for d, other in enumerate(p.ys() if along_y else p.xs()):
                if along_y:
                    part = mine.at[:, :, other, rows] if number == 1 else mine.at[p.x, :, other, rows]
                    copies.append((part, landing.at[d], p.at(y=other)))
                else:
                    part = mine.at[other, :, :, rows] if number == 1 else mine.at[other, :, p.y, rows]
                    copies.append((part, landing.at[d], p.at(x=other)))
        return [
            remote(src, dst, self.send.at[first + i], self.recv.at[first + i], device)
            for i, (src, dst, device) in enumerate(copies)
        ]

    def own_copy(self):
        return pltpu.make_async_copy(
            self.source.at[:, self.p.k, :, :, self.rows], self.mine.at[:, :, :, self.rows], self.fetch
        )

    def start(self, number):
        for copy in self.stage(number):
            copy.start()

    def begin(self):
        self.start(0)
        if self.fetch is not None:
            self.own_copy().start()

    def advance(self, number):
        p, rows, lay, mine = self.p, self.rows, self.p.lay, self.mine
        if number == 1 and self.fetch is not None:
            self.own_copy().wait()
        for copy in self.stage(number - 1):
            copy.wait_recv()
        if number == 1:

            def add(i, _):
                x, zy = i // (lay.Z * lay.Y), i % (lay.Z * lay.Y)
                z, y = zy // lay.Y, zy % lay.Y
                mine[x, z, y, rows] = (
                    mine[x, z, y, rows].astype(F32) + self.came[x, z, y, rows].astype(F32)
                ).astype(BF16)
                return 0

            lax.fori_loop(0, lay.X * lay.Z * lay.Y, add, 0)
        elif number == 2:
            outer = lay.X if self.y_first else lay.Z
            inner = lay.Z if self.y_first else lay.Y

            def add(i, _):
                a, b = i // inner, i % inner
                total = jnp.zeros((self.n, mine.shape[-1]), F32)
                for d in range(self.second.shape[0]):
                    total = total + self.second[d, a, b].astype(F32)
                if self.y_first:
                    mine[a, b, p.y, rows] = (mine[a, b, p.y, rows].astype(F32) + total).astype(BF16)
                else:
                    mine[p.x, a, b, rows] = (mine[p.x, a, b, rows].astype(F32) + total).astype(BF16)
                return 0

            lax.fori_loop(0, outer * inner, add, 0)
        elif number == 3:

            def add(z, _):
                total = mine[p.x, z, p.y, rows].astype(F32)
                for d in range(self.third.shape[0]):
                    total = total + self.third[d, z].astype(F32)
                mine[p.x, z, p.y, rows] = total.astype(BF16)
                return 0

            lax.fori_loop(0, lay.Z, add, 0)
        else:
            total = mine[p.x, p.z, p.y, rows].astype(F32)
            for d in range(lay.Z - 1):
                total = total + self.fourth[d].astype(F32)
            self.target[rows, :] = total
            return
        self.start(number)

    def sent(self):
        for number in range(4):
            for copy in self.stage(number):
                copy.wait_send()


def backward_kernel(
    lay, seqs, length, cuts, *refs
):
    (carry, ids, prev, tok_t, sums, q_hbm, k_hbm, v_hbm, given_hbm, full_in, pre, d_mix, d_up, d_down) = refs[:14]
    (tokens_grad, o_in, o_mix, o_up, o_down, o_sums) = refs[14:20]
    rest = list(refs[20:])
    (mask, tab, out_state, in_state, flags, key_part, value_part, grads, held, given_in, d_in, vec, vec_in,
     mine_mix, mine_up, mine_down, came_mix, came_up, came_down, came_in) = rest[:20]
    send, recv, misc_send, misc_recv, local = rest[-5:]
    landing = rest[20:-5]
    p = Place(lay)
    _, total_rows, width = held.shape
    q_in, k_in, v_in = held.at[0], held.at[1], held.at[2]
    pairs = width // 128
    total = seqs * pairs
    spot = local.shape[0] - 4
    loads = [
        pltpu.make_async_copy(src, dst, local.at[spot + i])
        for i, (src, dst) in enumerate(((q_hbm, q_in), (k_hbm, k_in), (v_hbm, v_in), (given_hbm, given_in)))
    ]
    for copy in loads:
        copy.start()
    p.barrier()

    groups, base, used = [], 0, 0
    for index, (source, mine, came, target, parts) in enumerate(
        (
            (d_down, mine_down, came_down, o_down, cuts[0]),
            (d_up, mine_up, came_up, o_up, cuts[1]),
            (d_mix, mine_mix, came_mix, o_mix, cuts[2]),
            (d_in, d_in.at[:, p.k], came_in, o_in, cuts[3]),
        )
    ):
        group = []
        for r0, n, y_first in parts:
            second, third, fourth = landing[3 * used : 3 * used + 3]
            fetch = local.at[used] if index < 3 else None
            group.append(
                Scatter(p, source, mine, came, second, third, fourth, target, r0, n, y_first, send, recv, base, fetch)
            )
            base += lay.hops
            used += 1
        groups.append(group)
    for group in groups[:3]:
        for flow in group:
            flow.begin()

    def pre_copy(b):
        return pltpu.make_async_copy(pre.at[pl.ds(b * 256, 256)], key_part.at[pl.ds(b * 256, 256)], misc_recv.at[2 + b])

    def grad_copy(b):
        return pltpu.make_async_copy(value_part.at[pl.ds(b * 256, 256)], tokens_grad.at[pl.ds(b * 256, 256)], misc_send.at[2 + b])

    blocks = total_rows // 256

    cos_a, sin_a, _, _ = angle_tables(length)
    cos_e, sin_e = edge_angles(cos_a, sin_a, length)
    for s in range(seqs):
        _, _, carried, last_mask, passes = seq_masks(ids, prev, s, length, p.c > 0)
        tab[s, 0] = cos_a * carried
        tab[s, 1] = sin_a * carried
        tab[s, 2] = cos_e * last_mask
        tab[s, 3] = sin_e * last_mask
        flags[s] = jnp.broadcast_to(passes, (8, 256))
    for copy in loads:
        copy.wait()

    def where(it):
        s, pair = it // pairs, it % pairs
        return s, pl.ds(pl.multiple_of(s * length, length), length), pl.ds(pl.multiple_of(pair * 128, 128), 128)

    def given_of(it):
        s, pair = it // pairs, it % pairs
        rows = pl.ds(pl.multiple_of(s * length, length), length)
        lane = lax.broadcasted_iota(jnp.int32, (1, 128), 1)
        plus = [given_in[rows, pl.ds(pl.multiple_of(pair * 256 + 128 * head, 128), 128)] for head in (0, 1)]
        given = plus[0] * lane_half(0).astype(BF16) + plus[1] * lane_half(1).astype(BF16)
        extra = jnp.zeros((length, 128), F32)
        for head in (0, 1):
            spare = 64 - 64 * head
            own = ((lane == spare) | (lane == spare + 1)).astype(F32)
            one = jnp.sum(plus[head].astype(F32) * own, axis=1, keepdims=True)
            extra = extra + one * lane_half(head)
        return plus, given, extra

    def local_state(it, _):
        s, rows, lanes = where(it)
        _, given, extra = given_of(it)
        queries, given = q_in[rows, lanes], given.astype(F32)
        scaled = jnp.concatenate([given * tab[s, 0], given * tab[s, 1]], axis=1).astype(BF16)
        state = dot(queries, scaled, TN)
        wide = queries.astype(F32) * extra
        for part in (0, 1):
            packed = pack_state(state[:, part * 128 : part * 128 + 128])
            out_state[it, 0:64, part * 128 : part * 128 + 128] = packed.astype(BF16)
            total_row = jnp.sum(wide * tab[s, part], axis=0, keepdims=True)
            out_state[it, 64:80, part * 128 : part * 128 + 128] = jnp.broadcast_to(total_row, (16, 128)).astype(BF16)
        return 0

    lax.fori_loop(0, total, local_state, 0)

    def chain_copy():
        return remote(out_state, in_state, misc_send.at[1], misc_recv.at[1], p.ring(-1))

    turn_c, turn_s = math.cos(OMEGA * length), math.sin(OMEGA * length)

    def hand_on():
        def one(it, _):
            came = in_state[it].astype(F32)
            came_c, came_s = came[:, 0:128], came[:, 128:256]
            turned = jnp.concatenate(
                [came_c * turn_c - came_s * turn_s, came_c * turn_s + came_s * turn_c], axis=1
            )
            state = out_state[it].astype(F32) + flags[it // pairs, 0:1, :] * turned
            out_state[it] = state.astype(BF16)
            return 0

        lax.fori_loop(0, total, one, 0)

    def chain_step():
        @pl.when(p.c == lay.C - 1)
        def _():
            in_state[...] = jnp.zeros_like(in_state)

        @pl.when(p.c < lay.C - 1)
        def _():
            chain_copy().wait_recv()
            hand_on()

        @pl.when(p.c > 0)
        def _():
            chain_copy().start()

    def line(number, group):
        return [functools.partial(flow.advance, number) for flow in groups[group]]

    order = [(1, 0), (1, 1), (2, 0), (1, 2), (2, 1), (3, 0), (2, 2), (3, 1), (4, 0), (3, 2), (4, 1), (4, 2)]
    thunks = [thunk for number, group in order for thunk in line(number, group)]
    inside = (len(thunks) * 2) // 3
    block = 256 if length % 256 == 0 else length

    def local_attention(it, _):
        @pl.when(it == ((lay.C - 1 - p.c) * total) // lay.C)
        def _():
            chain_step()

        for n, thunk in enumerate(thunks[:inside]):

            @pl.when(it == (n * total) // inside)
            def _(thunk=thunk):
                thunk()

        s, rows, lanes = where(it)
        for seq in range(seqs):

            @pl.when(it == seq * pairs)
            def _(seq=seq):
                row, column, _, _, _ = seq_masks(ids, prev, seq, length, p.c > 0)
                at_j = lax.broadcasted_iota(jnp.int32, (length, length), 0)
                at_i = lax.broadcasted_iota(jnp.int32, (length, length), 1)
                allowed = (column[:, 0:1] == row) & (at_j <= at_i)
                cos_a, sin_a, cos_r, sin_r = angle_tables(length)
                mask[...] = jnp.where(allowed, cos_a[:, 0:1] * cos_r + sin_a[:, 0:1] * sin_r, 0.0)

        lane = lax.broadcasted_iota(jnp.int32, (1, 128), 1)
        queries, keys, values = q_in[rows, lanes], k_in[rows, lanes], v_in[rows, lanes]
        plus, given, extra = given_of(it)
        query_total = jnp.zeros((length, 128), F32)
        for head in (0, 1):
            side = lane_half(head)
            only = side.astype(BF16)
            spare = 64 - 64 * head
            given_plus = plus[head]
            ones = ((lane == spare) | (lane == spare + 1)).astype(BF16)
            value_plus = values * only + ones
            key_only, query_only, given_only = keys * only, queries * only, given * only
            query_parts = []
            for b in range(length // block):
                lo = b * block
                scores = dot(key_only[lo : lo + block], queries[lo:], NT) * mask[lo : lo + block, lo:]
                grads_ji = (
                    dot(value_plus[lo : lo + block], given_plus[lo:], NT) * mask[lo : lo + block, lo:]
                ).astype(BF16)
                here = pl.ds(pl.multiple_of(s * length + lo, block), block)
                key_add = dot(grads_ji, query_only[lo:])
                value_add = dot(scores.astype(BF16), given_only[lo:])
                if head == 0:
                    key_part[here, lanes] = key_add
                    value_part[here, lanes] = value_add
                else:
                    key_part[here, lanes] += key_add
                    value_part[here, lanes] += value_add
                add = dot(grads_ji, key_only[lo : lo + block], TN)
                if lo:
                    query_total = jnp.concatenate([query_total[:lo], query_total[lo:] + add], axis=0)
                else:
                    query_total = query_total + add
        state_c, state_s = unpack_state(carry[it])
        wide = jnp.concatenate([state_c, state_s], axis=0).astype(BF16)
        reach = dot(given, wide, NT)
        totals = carry[it, 64:80, :].astype(F32)[0:1]
        query_total = query_total + tab[s, 0] * (reach[:, 0:128] + extra * totals[:, 0:128])
        query_total = query_total + tab[s, 1] * (reach[:, 128:256] + extra * totals[:, 128:256])
        grads[rows, lanes] = jnp.where(queries.astype(F32) > 0.0, query_total, 0.0).astype(BF16)
        return 0

    lax.fori_loop(0, total, local_attention, 0)

    def finish(it, _):
        s, rows, lanes = where(it)
        pair = it % pairs
        keys, values = k_in[rows, lanes], v_in[rows, lanes]
        state_c, state_s = unpack_state(in_state[it])
        by_row = jnp.concatenate([state_c, state_s], axis=0).astype(BF16)
        by_lane = jnp.concatenate([state_c, state_s], axis=1).astype(BF16)
        totals = in_state[it, 64:80, :].astype(F32)[0:1]
        c_j, s_j = tab[s, 2], tab[s, 3]
        key_reach = dot(values, by_row, NT) + totals
        value_reach = dot(keys, by_lane)
        key_grad = key_part[rows, lanes] + c_j * key_reach[:, 0:128] + s_j * key_reach[:, 128:256]
        value_grad = value_part[rows, lanes] + c_j * value_reach[:, 0:128] + s_j * value_reach[:, 128:256]
        key_lanes = pl.ds(pl.multiple_of(width + pair * 128, 128), 128)
        value_lanes = pl.ds(pl.multiple_of(2 * width + pair * 128, 128), 128)
        grads[rows, key_lanes] = jnp.where(keys.astype(F32) > 0.0, key_grad, 0.0).astype(BF16)
        grads[rows, value_lanes] = value_grad.astype(BF16)
        return 0

    lax.fori_loop(0, total, finish, 0)
    for b in range(blocks):
        pre_copy(b).start()
    thirds = [
        pltpu.make_async_copy(
            full_in.at[:, pl.ds(i * width, width)], held.at[i, pl.ds(0, width)], local.at[spot + i]
        )
        for i in range(3)
    ]
    for copy in thirds:
        copy.start()
    vec[0] = sums[...]

    def bias_sum(n, _):
        lanes = pl.ds(pl.multiple_of(n * 256, 256), 256)
        vec[0, 1:2, lanes] = rows_sum(grads[:, lanes].astype(F32))
        return 0

    lax.fori_loop(0, 3 * width // 256, bias_sum, 0)

    in_a, in_w = o_in.shape
    piece = math.lcm(in_w, 128)
    for n in range(3 * width // piece):
        for m in range(width // 256):
            part = dot(tok_t[m * 256 : (m + 1) * 256, :], grads[:, n * piece : (n + 1) * piece]).astype(BF16)
            for i in range(piece // in_w):
                c = n * (piece // in_w) + i
                lo = m * 256
                while lo < (m + 1) * 256:
                    r = lo // in_a
                    hi = min((r + 1) * in_a, (m + 1) * 256)
                    d_in[c // 2, c % 2, r // lay.Y, r % lay.Y, lo - r * in_a : hi - r * in_a, :] = part[
                        lo - m * 256 : hi - m * 256, i * in_w : (i + 1) * in_w
                    ]
                    lo = hi
    for flow in groups[3]:
        flow.begin()

    def vector_stage(number):
        first = (0, 1, lay.X, lay.X + lay.Y - 1)[number]
        peers = (
            [p.at(k=1 - p.k)],
            [p.at(x=x) for x in p.xs()],
            [p.at(y=y) for y in p.ys()],
            [p.at(z=z) for z in p.zs()],
        )[number]
        shift = 2 + blocks + first
        return [
            remote(vec.at[number], vec_in.at[first + i], misc_send.at[shift + i], misc_recv.at[shift + i], peer)
            for i, peer in enumerate(peers)
        ]

    def vector_start(number):
        for copy in vector_stage(number):
            copy.start()

    def vector_add(number):
        total_vec = vec[number]
        first = (0, 1, lay.X, lay.X + lay.Y - 1)[number]
        for i, copy in enumerate(vector_stage(number)):
            copy.wait_recv()
            total_vec = total_vec + vec_in[first + i]
        if number == 3:
            o_sums[...] = total_vec
        else:
            vec[number + 1] = total_vec
            vector_start(number + 1)

    vector_start(0)
    for thunk in thunks[inside:]:
        thunk()
    tail = []
    for number in (1, 2, 3, 4):
        tail += line(number, 3)
        tail.append(functools.partial(vector_add, number - 1))
    done = 0
    for copy in thirds:
        copy.wait()
    for b in range(blocks):
        pre_copy(b).wait()
        part = slice(b * 256, (b + 1) * 256)
        out = key_part[part, :]
        for i in range(3):
            out = out + dot(grads[part, i * width : (i + 1) * width], held[i, 0:width, :], NT)
        value_part[part, :] = out
        grad_copy(b).start()
        upto = (len(tail) * (b + 1)) // (blocks + 1)
        for thunk in tail[done:upto]:
            thunk()
        done = upto
    for thunk in tail[done:]:
        thunk()
    for b in range(blocks):
        grad_copy(b).wait()
    for group in groups:
        for flow in group:
            flow.sent()
    for number in range(4):
        for copy in vector_stage(number):
            copy.wait_send()

    @pl.when(p.c > 0)
    def _():
        chain_copy().wait_send()


def backward(lay, ids, prev, q, k, v, given, carry, tok_t, full_in, sums, pre, d_mix, d_up, d_down, in_shape):
    seqs, length = ids.shape
    rows, width = q.shape
    total = seqs * (width // 128)
    in_slots = (lay.X, 2, lay.Z, lay.Y) + in_shape
    sources = (d_down, d_up, d_mix, in_slots)
    slots = [s if isinstance(s, tuple) else s.shape for s in sources]
    cuts = tuple(pieces(s[4], 1) for s in slots)
    landing = []
    for slot, parts in zip(slots, cuts, strict=True):
        for _, n, y_first in parts:
            tile = (n, slot[5])
            if y_first:
                landing += [(lay.Y - 1, lay.X, lay.Z) + tile, (lay.X - 1, lay.Z) + tile]
            else:
                landing += [(lay.X - 1, lay.Z, lay.Y) + tile, (lay.Y - 1, lay.Z) + tile]
            landing.append((lay.Z - 1,) + tile)
    flows = sum(len(c) for c in cuts)
    vmem, anyspace = pl.BlockSpec(memory_space=pltpu.VMEM), pl.BlockSpec(memory_space=pl.ANY)
    shape = jax.ShapeDtypeStruct
    ff = sums.shape[1]
    blocks = rows // 256
    half = [(s[0],) + s[2:] for s in slots]
    hop = lay.hops
    misc = 2 + blocks + hop
    scratch = [
        pltpu.VMEM((length, length), F32),
        pltpu.VMEM((seqs, 4, length, 128), F32),
        pltpu.VMEM((total, 80, 256), BF16),
        pltpu.VMEM((total, 80, 256), BF16),
        pltpu.VMEM((seqs, 8, 256), F32),
        pltpu.VMEM((rows, width), F32),
        pltpu.VMEM((rows, width), F32),
        pltpu.VMEM((rows, 3 * width), BF16),
        pltpu.VMEM((3, rows, width), BF16),
        pltpu.VMEM((rows, 2 * width), BF16),
        pltpu.VMEM(in_slots, BF16),
        pltpu.VMEM((4, 4, ff), F32),
        pltpu.VMEM((hop, 4, ff), F32),
    ]
    scratch += [pltpu.VMEM(half[i], BF16) for i in (2, 1, 0)] + [pltpu.VMEM(half[i], BF16) for i in (2, 1, 0, 3)]
    scratch += [pltpu.VMEM(s, BF16) for s in landing]
    scratch += [
        pltpu.SemaphoreType.DMA((flows * hop,)),
        pltpu.SemaphoreType.DMA((flows * hop,)),
        pltpu.SemaphoreType.DMA((misc,)),
        pltpu.SemaphoreType.DMA((misc,)),
        pltpu.SemaphoreType.DMA((flows + 4,)),
    ]
    return pl.pallas_call(
        functools.partial(backward_kernel, lay, seqs, length, cuts),
        out_shape=[shape((rows, width), F32)]
        + [shape(slots[i][4:], F32) for i in (3, 2, 1, 0)]
        + [shape((4, ff), F32)],
        in_specs=[vmem] * 5 + [anyspace] * 9,
        out_specs=[anyspace] + [vmem] * 5,
        scratch_shapes=scratch,
        compiler_params=pltpu.CompilerParams(
            collective_id=1, has_side_effects=True, vmem_limit_bytes=VMEM_LIMIT
        ),
        name="backward_attention",
    )(carry, ids, prev, tok_t, sums, q, k, v, given, full_in, pre, d_mix, d_up, d_down)


def per_device(
    tokens, segment_ids, in_weight, in_bias, mix_weight, mix_bias, first_gain, first_shift,
    up_weight, up_bias, down_weight, down_bias, second_gain, second_shift, cotangent,
):
    lay = Layout(lax.axis_size("row"), lax.axis_size("col"))
    seqs, length, width = tokens.shape
    flat = tokens.reshape(seqs * length, width)
    line = lambda v: v.astype(F32)[None]
    q, k, v, att, den, carry, prev, full_in, g_mix, g_up, g_down = forward(
        lay, flat, segment_ids, line(in_bias), (in_weight, mix_weight, up_weight, down_weight.T)
    )
    vectors = [line(u) for u in (mix_bias, up_bias, down_bias, first_gain, first_shift, second_gain, second_shift)]
    layer_out, pre, given, tok_t, d_mix, d_up, d_down, sums = dense(
        lay, flat, att, den, cotangent.reshape(seqs * length, width), vectors, g_mix, g_up, g_down
    )
    tokens_grad, o_in, o_mix, o_up, o_down, o_sums = backward(
        lay, segment_ids, prev, q, k, v, given, carry, tok_t, full_in, sums, pre, d_mix, d_up, d_down,
        in_weight.shape,
    )
    part = lambda row, n: o_sums[row, n * width : (n + 1) * width]
    return (
        layer_out.reshape(tokens.shape),
        tokens_grad.reshape(tokens.shape),
        o_in,
        o_sums[1, : 3 * width],
        o_mix,
        part(2, 0),
        part(2, 1),
        part(2, 2),
        o_up,
        o_sums[0],
        o_down.T,
        part(2, 3),
        part(3, 0),
        part(3, 1),
    )


def solution(mesh):
    block, matrix, rep = P("row", "col", None), P("row", "col"), P()
    return jax.shard_map(
        per_device,
        mesh=mesh,
        in_specs=(block, matrix, matrix, rep, matrix, rep, rep, rep, matrix, rep, matrix, rep, rep, rep, block),
        out_specs=(block, block, matrix, rep, matrix, rep, rep, rep, matrix, rep, matrix, rep, rep, rep),
        check_vma=False,
    )
```

time: 1130 us -> 320 us (0.28); the launches traced: 1110 us -> 319 us
  waiting for transfers between devices: 392 us -> 0 us
  matrix products: 364 us -> 0 us
  Pallas kernels: 0 us -> 297 us
  local copies, waits for them, and re-layouts: 151 us -> 19.7 us
  blocking collectives: 109 us -> 0 us
  other arithmetic: 77.7 us -> 1.29 us
  between operations: 15.8 us -> 0.68 us
    dot_general x147 -> x0, matrix products: 364 us -> none  [the longest x4 39.3 us: right_product(): lax.dot_general(first, second, (((1,), (1,)), ((), ())), preferred_elemen...]
    pallas_call x0 -> x3, Pallas kernels: none -> 297 us  [the longest x1 120 us: backward(): pl.pallas_call(functools.partial(backward_kernel, lay, seqs, length, cuts...]
    reduce_scatter x5 -> x0, waiting for transfers between devices: 174 us -> none  [the longest x1 65 us: reduce_weights(): lax.psum_scatter(partial_value[2].astype(jnp.bfloat16), 'row', scatter_di...]
    unnamed x17 -> x0, waiting for transfers between devices: 143 us -> none
    all_gather x6 -> x0, waiting for transfers between devices: 74.6 us -> none  [the longest x1 53.4 us: fetch_weights(): lax.all_gather(partial_value[0], 'row', axis=0, tiled=True)]
    unnamed x148 -> x13, local copies, waits for them, and re-layouts: 69.2 us -> 6.61 us
    all_gather x6 -> x0, blocking collectives: 50.4 us -> none  [the longest x1 13.1 us: fetch_weights(): lax.all_gather(up_weight, 'col', axis=1, tiled=True)]
    psum x1 -> x0, blocking collectives: 40.9 us -> none  [per_device(): lax.psum((in_bias_grad, mix_bias_grad, first_gain_grad, first_shift_grad,...]
  transfers between devices with their start and end apart: 14 -> 0, of which waited for: 9 -> 0; matrix products, arithmetic and copies ran while one was open for 42% -> 0% of each run, Pallas kernels for 0% -> 0%
where the time goes in v1:
time: 320 us; the launch traced here: 319 us
  Pallas kernels  297 us (93%)
  local copies, waits for them, and re-layouts  19.7 us (6%)
    pallas_call x1, Pallas kernels, backward(): pl.pallas_call(functools.partial(backward_kernel, lay, seqs, length, cuts...  120 us
    pallas_call x1, Pallas kernels, forward(): pl.pallas_call(functools.partial(forward_kernel, lay, seqs, length, cuts)...  108 us
    pallas_call x1, Pallas kernels, dense(): pl.pallas_call(functools.partial(dense_kernel, lay, row_blocks, chunk, di...  69 us
    broadcast_in_dim x7, local copies, waits for them, and re-layouts, per_device(): line = lambda v: v.astype(F32)[None]  8.86 us
    unnamed x13, local copies, waits for them, and re-layouts  6.61 us

profile of v1, /device:TPU:0, one launch (start us, length us, event | category | flops | bytes accessed | tf_op | source)
XLA Modules:
  0.0 319.1 jit_solution(14945585318787311598)
XLA Ops:
  0.6 1.3 reshape.45.mix_b
  1.9 1.3 reshape.48.gain1
  3.2 1.3 reshape.49.shift1
  4.4 1.3 reshape.47.down_b
  5.7 1.3 reshape.50.gain2
  7.0 1.3 reshape.51.shift2
  8.2 1.3 reshape.44.bias
  9.5 1.3 broadcast_in_dim.58
  10.8 108.4 %forward_attention.1 = (bf16[1024,768]{1,0:T(8,128)(2,1)}, bf16[1024,768]{1,0:T(8,128)(2,1)}, bf16[1024,768]{1,0:T(8,128)(2,1)}, f32[1024,768]{1,0:T(8,128)}, f3...) custom-call(bf16[1024,768]{1,0:T(8,128)(2,1)} %bitcast.8, ...), custom_call_target="tpu_custom_call" | custom-call | tf_op jit(solution)/shard_map/forward_attention/pallas_call | solution.py:430
  119.2 69.0 %dense.1 = (bf16[1024,768]{1,0:T(8,128)(2,1)}, f32[1024,768]{1,0:T(8,128)}, bf16[1024,1536]{1,0:T(8,128)(2,1)}, bf16[768,1024]{1,0:T(8,128)(2,1)}, bf16[2,2,4,2,...) custom-call(bf16[1024,768]{1,0:T(8,128)(2,1)} %bitcast.9, ...), custom_call_target="tpu_custom_call" | custom-call | tf_op jit(solution)/shard_map/dense/pallas_call | solution.py:650
  188.2 120.0 %backward_attention.1 = (f32[1024,768]{1,0:T(8,128)}, f32[96,576]{1,0:T(8,128)}, f32[96,192]{1,0:T(8,128)}, f32[96,768]{1,0:T(8,128)}, f32[192,384]{1,0:T(8,128)}, /*index=5*/f32[4,3072]{1,0:T(4,128)}) custom-call(bf16[12,80,256]{2,1,0:T(8,128)(2,1)} %get-tuple-element.45.refs_0_, s32[2,512]{1,0:T(2,128)} %refs_1_.1, s32[2,512]{1,0:T(2,128)} %get-tuple-element.46.refs_2_, ...), custom_call_target="tpu_custom_call" | custom-call | tf_op jit(solution)/shard_map/backward_attention/pallas_call | solution.py:1183
  308.2 1.4 slice.28
  309.6 1.4 slice_reduce_fusion
  311.0 1.5 slice_reduce_fusion.1
  312.5 0.0 copy-start.2
  312.5 0.0 copy-start.3
  312.5 0.0 copy-start.1
  312.5 0.0 copy-start
  312.5 3.8 %copy.34 = f32[2,512,768]{2,1,0:T(8,128)} copy(f32[2,512,768]{2,1,0:T(8,128)} %bitcast.11) | data formatting | bytes 6291456
  316.3 0.0 copy-done.2
  316.3 0.7 copy.35
  317.0 0.0 copy-done.3
  317.0 0.6 copy.36
  317.6 0.0 copy-done.1
  317.6 0.7 copy.37
  318.4 0.0 copy-done
  318.4 0.7 copy.38
Async XLA Ops:
  312.5 3.8 %copy-start.2 = (f32[96,576]{1,0:T(8,128)S(1)}, f32[96,576]{1,0:T(8,128)}, u32[]{:S(2)}) copy-start(f32[96,576]{1,0:T(8,128)} %get-tuple-element.86) | copy-start | bytes 663556
  312.5 4.5 %copy-start.3 = (f32[96,192]{1,0:T(8,128)S(1)}, f32[96,192]{1,0:T(8,128)}, u32[]{:S(2)}) copy-start(f32[96,192]{1,0:T(8,128)} %get-tuple-element.88) | copy-start | bytes 221188
  312.5 5.2 %copy-start.1 = (f32[96,768]{1,0:T(8,128)S(1)}, f32[96,768]{1,0:T(8,128)}, u32[]{:S(2)}) copy-start(f32[96,768]{1,0:T(8,128)} %get-tuple-element.92) | copy-start | bytes 884740
  312.5 5.9 %copy-start = (f32[192,384]{1,0:T(8,128)S(1)}, f32[192,384]{1,0:T(8,128)}, u32[]{:S(2)}) copy-start(f32[192,384]{1,0:T(8,128)} %get-tuple-element.63) | copy-start | bytes 884740

commit v2 on v1

--- a/solution.py
+++ b/solution.py
@@ -126,8 +126,8 @@
         self.arrive(number - 1)
         self.start(number)
 
-    def sent(self):
-        for number in range(4):
+    def sent(self, numbers):
+        for number in numbers:
             for copy in self.stage(number):
                 copy.wait_send()
 
@@ -166,9 +166,9 @@
 
 
 def angle_tables(length):
-    column = lax.broadcasted_iota(jnp.int32, (length, 128), 0).astype(F32) * OMEGA
     row = lax.broadcasted_iota(jnp.int32, (1, length), 1).astype(F32) * OMEGA
-    return jnp.cos(column), jnp.sin(column), jnp.cos(row), jnp.sin(row)
+    rows = jnp.cos(row), jnp.sin(row)
+    return *(jnp.transpose(jnp.broadcast_to(r, (128, length))) for r in rows), *rows
 
 
 def edge_angles(cosine, sine, length):
@@ -205,16 +205,22 @@
 
 
 def forward_kernel(
-    lay, seqs, length, cuts,
-    tokens, ids, bias, in_s, mix_s, up_s, down_s,
-    q_out, k_out, v_out, att, den, carry, prev, full_in, g_mix, g_up, g_down,
-    g_in, mask, tab, out_state, flags,
+    lay, seqs, length, cuts, split,
+    tokens, ids, bias_in, in_s, mix_s, up_s, down_s,
+    att, den, carry, prev, q_hbm, k_hbm, v_hbm, in_hbm, mix_hbm, tok_hbm, g_up, g_down,
+    q_out, k_out, v_out, full_in, full_mix, tok_t, g_in, g_mix, bias, mask, tab, out_state, flags,
     send, recv, misc_send, misc_recv, local,
 ):
     p = Place(lay)
     pairs = q_out.shape[1] // 128
     width = q_out.shape[1]
     total = seqs * pairs
+    outputs = [
+        pltpu.make_async_copy(src, dst, local.at[4 + i])
+        for i, (src, dst) in enumerate(
+            ((q_out, q_hbm), (k_out, k_hbm), (v_out, v_hbm), (full_in, in_hbm), (tok_t, tok_hbm), (full_mix, mix_hbm))
+        )
+    ]
     p.barrier()
     flows = []
     base = 0
@@ -244,6 +250,9 @@
         copy.wait()
     for flow in groups[0]:
         flow.advance(1)
+    tok_t[...] = jnp.transpose(tokens[...])
+    bias[...] = bias_in[...].astype(F32).reshape(bias.shape)
+    outputs[4].start()
 
     cos_a, sin_a, cos_r, sin_r = angle_tables(length)
     cos_e, sin_e = edge_angles(cos_a, sin_a, length)
@@ -265,7 +274,14 @@
             flow.advance(number)
     for flow in groups[0]:
         flow.arrive(3)
+
+    def onward(number, group):
+        for flow in groups[group]:
+            flow.advance(number)
+
+    onward(1, 1)
     unslot(g_in, full_in, lay, in_s.shape[0], in_s.shape[1], False)
+    outputs[3].start()
 
     blocks = width // 256
     half = tokens.shape[0] // 2
@@ -283,9 +299,10 @@
 
         lax.fori_loop(0, blocks, column_block, 0)
 
-    project(q_out, 0, True)
     project(k_out, width, True)
+    onward(1, 2)
     project(v_out, 2 * width, False)
+    during = [(2, 1), (2, 2), (3, 1)] if split else [(2, 1), (2, 2), (1, 3), (3, 1)]
 
     def where(it):
         s, pair = it // pairs, it % pairs
@@ -338,27 +355,24 @@
         def _():
             chain_copy().start()
 
-    def fine(number):
-        return [functools.partial(f.advance, number) for f in groups[1]], [
-            functools.partial(f.advance, number) for f in groups[2]
-        ], [functools.partial(f.advance, number) for f in groups[3]]
-
-    m1, u1, d1 = fine(1)
-    m2, u2, d2 = fine(2)
-    m3, u3, d3 = fine(3)
-    thunks = m1 + u1 + m2 + m3 + d1 + u2 + d2 + u3 + d3
+    pl.when(p.c == 0)(chain_step)
+    project(q_out, 0, True)
+    for copy in outputs[:3]:
+        copy.start()
+    pl.when(p.c == 1)(chain_step)
     step_block = 256 if length % 256 == 0 else length
+    chain_turn = (total * 2) // 3 + ((p.c - 2) * (total // 3)) // max(lay.C - 2, 1)
 
     def local_attention(it, _):
-        @pl.when(it == (p.c * total) // lay.C)
+        @pl.when((it == chain_turn) & (p.c > 1))
         def _():
             chain_step()
 
-        for n, thunk in enumerate(thunks):
-
-            @pl.when(it == (n * total) // len(thunks))
-            def _(thunk=thunk):
-                thunk()
+        for n, (number, group) in enumerate(during):
+
+            @pl.when(it == (n * total) // len(during))
+            def _(number=number, group=group):
+                onward(number, group)
 
         s, rows, lanes = where(it)
         low, high = lane_half(0), lane_half(1)
@@ -399,19 +413,28 @@
         return 0
 
     lax.fori_loop(0, total, finish, 0)
-
-    for flow in flows[len(groups[0]) :]:
+    for number, group in [(3, 2)] if split else [(3, 2), (2, 3), (3, 3)]:
+        onward(number, group)
+    for flow in groups[1]:
         flow.arrive(3)
+    unslot(g_mix, full_mix, lay, mix_s.shape[0], mix_s.shape[1], False)
+    outputs[5].start()
+    for flow in groups[2]:
+        flow.arrive(3)
+    for flow in groups[3]:
+        flow.arrive(0 if split else 3)
     for flow in flows:
-        flow.sent()
+        flow.sent(range(1) if split and flow in groups[3] else range(4))
     ring_ids.wait_send()
+    for copy in outputs:
+        copy.wait()
 
     @pl.when(p.c < lay.C - 1)
     def _():
         chain_copy().wait_send()
 
 
-def forward(lay, tokens, ids, bias, shards):
+def forward(lay, tokens, ids, bias, shards, split):
     seqs, length = ids.shape
     rows, width = tokens.shape
     total = seqs * (width // 128)
@@ -421,19 +444,22 @@
     vmem, anyspace = pl.BlockSpec(memory_space=pltpu.VMEM), pl.BlockSpec(memory_space=pl.ANY)
     slots = [(lay.X, 2, lay.Z, lay.Y) + s.shape for s in shards]
     shape = jax.ShapeDtypeStruct
+    copied = [(rows, width)] * 3 + [(width, 3 * width), (width, width), (width, rows)]
     outs = (
-        [shape((rows, width), BF16)] * 3
-        + [shape((rows, width), F32)] * 2
-        + [shape((total, 80, 256), BF16), shape(ids.shape, jnp.int32), shape((width, 3 * width), BF16)]
-        + [shape(s, BF16) for s in slots[1:]]
+        [shape((rows, width), F32)] * 2
+        + [shape((total, 80, 256), BF16), shape(ids.shape, jnp.int32)]
+        + [shape(s, BF16) for s in copied + slots[2:]]
     )
     return pl.pallas_call(
-        functools.partial(forward_kernel, lay, seqs, length, cuts),
+        functools.partial(forward_kernel, lay, seqs, length, cuts, split),
         out_shape=outs,
         in_specs=[vmem] * 7,
-        out_specs=[vmem] * 8 + [anyspace] * 3,
-        scratch_shapes=[
+        out_specs=[vmem] * 4 + [anyspace] * 8,
+        scratch_shapes=[pltpu.VMEM(s, BF16) for s in copied]
+        + [
             pltpu.VMEM(slots[0], BF16),
+            pltpu.VMEM(slots[1], BF16),
+            pltpu.VMEM((1, 3 * width), F32),
             pltpu.VMEM((seqs, length, length), F32),
             pltpu.VMEM((seqs, 4, length, 128), F32),
                 pltpu.VMEM((total, 80, 256), BF16),
@@ -442,7 +468,7 @@
             pltpu.SemaphoreType.DMA((flows * lay.hops,)),
             pltpu.SemaphoreType.DMA((2,)),
             pltpu.SemaphoreType.DMA((2,)),
-            pltpu.SemaphoreType.DMA((4,)),
+            pltpu.SemaphoreType.DMA((10,)),
         ],
         compiler_params=pltpu.CompilerParams(
             collective_id=0, has_side_effects=True, vmem_limit_bytes=VMEM_LIMIT
@@ -470,24 +496,31 @@
 
 
 def dense_kernel(
-    lay, row_blocks, chunk, direct,
-    tokens, att, den, cot, mix_b, up_b, down_b, gain1, shift1, gain2, shift2, g_mix, g_up, g_down,
-    layer_out, pre_out, given_out, tok_t, d_mix, d_up, d_down, sums,
-    w_mix, w_up, w_down, mix_raw, act, up_g, hid_t, down_t, att_t, mix_g, slope, acc, sem,
+    lay, row_blocks, chunk, split, cuts, *refs
 ):
+    tokens, att, den, cot = refs[:4]
+    given_vectors = refs[4:11]
+    w_mix_in, g_up, g_down = refs[11:14]
+    layer_out, pre_out, given_out, d_mix, d_up, d_down_out, sums = refs[14:21]
+    rest = refs[21:]
+    if split:
+        g_down, rest = rest[0], rest[1:]
+    (w_mix, w_up, w_down, act, up_g, hid_t, down_t, att_t, mix_g, unit_v, scale_v, grad_v, vectors, acc, sem) = rest[:15]
     step = pl.program_id(0)
     block, width = tokens.shape
     ff = act.shape[1]
     chunks = ff // chunk
-    mix_a, mix_w = d_mix.shape[-2:]
-    up_w = d_up.shape[-1]
-    down_a, down_w = d_down.shape[-2:]
+    mix_w, up_w = d_mix.shape[-1], d_up.shape[-1]
+    down_a, down_w = g_down.shape[-2:] if split else d_down_out.shape[-2:]
+    mix_b, down_b, gain1, shift1, gain2, shift2 = [vectors.at[i : i + 1, 0:width] for i in range(1, 7)]
+    starts = [0, row_blocks, 2 * row_blocks, 2 * row_blocks + lay.Z, 3 * row_blocks + lay.Z]
+    last_step = 3 * row_blocks + 2 * lay.Z - 1
 
     def fetch_mix():
-        return [pltpu.make_async_copy(g_mix, mix_raw, sem.at[0])]
+        return [pltpu.make_async_copy(w_mix_in, w_mix, sem.at[0])]
 
     def fetch_up():
-        if not direct:
+        if not split:
             return [pltpu.make_async_copy(g_up, w_up, sem.at[1])]
         return [
             pltpu.make_async_copy(g_up.at[c // 2, c % 2], w_up.at[:, :, :, pl.ds(c * up_w, up_w)], sem.at[3 + c])
@@ -495,7 +528,7 @@
         ]
 
     def fetch_down():
-        if not direct:
+        if not split:
             return [pltpu.make_async_copy(g_down, w_down, sem.at[2])]
         return [
             pltpu.make_async_copy(
@@ -507,6 +540,21 @@
             for r in range(lay.R)
         ]
 
+    if split:
+        d_down, came, landing = rest[15], rest[16], rest[17:-4]
+        send, recv, send2, recv2 = rest[-4:]
+        p = Place(lay)
+        gathers, scatters = [], []
+        for n, (r0, size, y_first) in enumerate(cuts):
+            gathers.append(Gather(p, None, g_down, r0, size, y_first, send, recv, n * lay.hops))
+            scatters.append(
+                Scatter(
+                    p, d_down, d_down.at[:, p.k], came, landing[n], None, None, None,
+                    r0, size, y_first, send2, recv2, n * lay.hops, None,
+                )
+            )
+        out_copy = pltpu.make_async_copy(d_down.at[:, p.k], d_down_out, sem.at[1])
+
     def up_chunk(lanes):
         return w_up[:, :, :, lanes].reshape(width, chunk)
 
@@ -515,59 +563,144 @@
 
     @pl.when(step == 0)
     def _():
-        for copy in fetch_mix() + fetch_up() + fetch_down():
+        for copy in fetch_mix() + fetch_up() + ([] if split else fetch_down()):
             copy.start()
+        if split:
+            p.barrier()
+            for flow in gathers:
+                flow.start(1)
+        for i, vector in enumerate(given_vectors):
+            vectors[i : i + 1, 0 : vector.shape[0]] = vector[...].astype(F32).reshape(1, vector.shape[0])
         acc[...] = jnp.zeros_like(acc)
         for copy in fetch_mix():
             copy.wait()
-        unslot(mix_raw, w_mix, lay, mix_a, mix_w, False)
-
-    @pl.when(step < row_blocks)
+
+    @pl.when(step < starts[1])
     def _():
         rows = pl.ds(pl.multiple_of(step * block, block), block)
         att_low = att[...].astype(BF16)
         att_t[:, rows] = jnp.transpose(att_low)
-        tok_t[...] = jnp.transpose(tokens[...])
         mixed = dot(att_low, w_mix[...]) + mix_b[...]
         unit1, scale1 = normalize(tokens[...].astype(F32) + mixed)
-        hidden = unit1 * gain1[...] + shift1[...]
-        hidden_low = hidden.astype(BF16)
+        unit_v[rows, :] = unit1
+        scale_v[rows, :] = jnp.broadcast_to(scale1, (block, 128))
+        hidden_low = (unit1 * gain1[...] + shift1[...]).astype(BF16)
         hid_t[:, rows] = jnp.transpose(hidden_low)
 
         @pl.when(step == 0)
         def _():
-            for copy in fetch_up() + fetch_down():
+            for copy in fetch_up():
                 copy.wait()
 
-        def up_down(n, total):
+        def up_part(n, _):
             lanes = pl.ds(pl.multiple_of(n * chunk, chunk), chunk)
-            up = dot(hidden_low, up_chunk(lanes)) + up_b[:, lanes]
+            up = dot(hidden_low, up_chunk(lanes)) + vectors[0:1, lanes]
             cdf = 0.5 + 0.5 * lax.erf(up * math.sqrt(0.5))
             density = jnp.exp(up * up * -0.5) * (1.0 / math.sqrt(2.0 * math.pi))
-            slope[:, lanes] = cdf + up * density
-            active = (up * cdf).astype(BF16)
-            act[rows, lanes] = active
-            return total + dot(active, down_chunk(lanes), NT)
-
-        down = lax.fori_loop(0, chunks, up_down, jnp.zeros((block, width), F32)) + down_b[...]
+            up_g[rows, lanes] = (cdf + up * density).astype(BF16)
+            act[rows, lanes] = (up * cdf).astype(BF16)
+            if split:
+
+                @pl.when((step == 1) & (n == 1))
+                def _():
+                    for flow in gathers:
+                        flow.advance(2)
+
+                @pl.when((step == starts[1] - 1) & (n == 1))
+                def _():
+                    for flow in gathers:
+                        flow.advance(3)
+
+            return 0
+
+        lax.fori_loop(0, chunks, up_part, 0)
+
+    if split:
+
+        @pl.when(step == starts[1] - 1)
+        def _():
+            for flow in gathers:
+                flow.arrive(3)
+            for copy in fetch_down():
+                copy.start()
+
+    @pl.when(step == starts[1])
+    def _():
+        for copy in fetch_down():
+            copy.wait()
+
+    @pl.when((step >= starts[1]) & (step < starts[2]))
+    def _():
+        rows = pl.ds(pl.multiple_of((step - starts[1]) * block, block), block)
+
+        def down_part(n, total):
+            lanes = pl.ds(pl.multiple_of(n * chunk, chunk), chunk)
+            return total + dot(act[rows, lanes], down_chunk(lanes), NT)
+
+        down = lax.fori_loop(0, chunks, down_part, jnp.zeros((block, width), F32)) + down_b[...]
+        hidden = unit_v[rows, :] * gain1[...] + shift1[...]
         unit2, scale2 = normalize(hidden + down)
         layer_out[...] = (unit2 * gain2[...] + shift2[...]).astype(BF16)
         given = cot[...]
         acc[3:4, 0:width] += rows_sum(given * unit2)
         acc[3:4, width : 2 * width] += rows_sum(given)
         sum_grad = normalize_grad(given * gain2[...], unit2, scale2)
+        grad_v[rows, :] = sum_grad
         down_grad = sum_grad.astype(BF16)
         down_t[:, rows] = jnp.transpose(down_grad)
         acc[2:3, 3 * width : 4 * width] += rows_sum(down_grad.astype(F32))
 
+    @pl.when((step >= starts[2]) & (step < starts[3]))
+    def _():
+        n = step - starts[2]
+        lanes = pl.ds(pl.multiple_of(n * chunk, chunk), chunk)
+        part = dot(down_t[...], act[:, lanes]).astype(BF16)
+        for c in range(lay.C):
+            for y in range(lay.Y):
+                tile = part[c * down_a : (c + 1) * down_a, y * down_w : (y + 1) * down_w]
+                if split:
+                    d_down[c // 2, c % 2, n, y] = tile
+                else:
+                    d_down_out[c // 2, c % 2, 0, y] = tile
+
+    if split:
+
+        @pl.when(step == starts[3])
+        def _():
+            for flow in scatters:
+                flow.start(0)
+
+        @pl.when(step == starts[3] + 1)
+        def _():
+            for flow in scatters:
+                flow.advance(1)
+
+        @pl.when(step == last_step)
+        def _():
+            for flow in scatters:
+                flow.add(2)
+            out_copy.start()
+            for flow in gathers:
+                flow.sent(range(1, 4))
+            for flow in scatters:
+                flow.sent(range(2))
+            out_copy.wait()
+
+    @pl.when((step >= starts[3]) & (step < starts[4]))
+    def _():
+        rows = pl.ds(pl.multiple_of((step - starts[3]) * block, block), block)
+        sum_grad = grad_v[rows, :]
+        down_grad = sum_grad.astype(BF16)
+
         def back(n, total):
             lanes = pl.ds(pl.multiple_of(n * chunk, chunk), chunk)
-            grad = (dot(down_grad, down_chunk(lanes)) * slope[:, lanes]).astype(BF16)
+            grad = (dot(down_grad, down_chunk(lanes)) * up_g[rows, lanes].astype(F32)).astype(BF16)
             up_g[rows, lanes] = grad
             acc[0:1, lanes] += rows_sum(grad.astype(F32))
             return total + dot(grad, up_chunk(lanes), NT)
 
         hidden_grad = lax.fori_loop(0, chunks, back, sum_grad)
+        unit1, scale1 = unit_v[rows, :], scale_v[rows, 0:1]
         acc[2:3, width : 2 * width] += rows_sum(hidden_grad * unit1)
         acc[2:3, 2 * width : 3 * width] += rows_sum(hidden_grad)
         pre_grad = normalize_grad(hidden_grad * gain1[...], unit1, scale1)
@@ -601,94 +734,110 @@
                 at = t * 256 + head * 128
                 given_out[:, at : at + 128] = both.astype(BF16)
 
-    @pl.when(step >= row_blocks)
+    @pl.when(step >= starts[4])
     def _():
-        n = step - row_blocks
+        n = step - starts[4]
         lanes = pl.ds(pl.multiple_of(n * chunk, chunk), chunk)
-        up_part = dot(hid_t[...], up_g[:, lanes]).astype(BF16)
+        part = dot(hid_t[...], up_g[:, lanes]).astype(BF16)
         for i in range(chunk // up_w):
-            d_up[i // 2, i % 2] = up_part[:, i * up_w : (i + 1) * up_w].reshape(d_up.shape[2:])
-        down_part = dot(down_t[...], act[:, lanes]).astype(BF16)
+            d_up[i // 2, i % 2] = part[:, i * up_w : (i + 1) * up_w].reshape(d_up.shape[2:])
+
+    @pl.when(step == starts[4])
+    def _():
+        part = dot(att_t[...], mix_g[...]).astype(BF16)
         for c in range(lay.C):
-            for y in range(lay.Y):
-                d_down[c // 2, c % 2, 0, y] = down_part[
-                    c * down_a : (c + 1) * down_a, y * down_w : (y + 1) * down_w
-                ]
-
-    @pl.when(step == row_blocks)
-    def _():
-        mix_part = dot(att_t[...], mix_g[...]).astype(BF16)
-        for c in range(lay.C):
-            d_mix[c // 2, c % 2] = mix_part[:, c * mix_w : (c + 1) * mix_w].reshape(d_mix.shape[2:])
+            d_mix[c // 2, c % 2] = part[:, c * mix_w : (c + 1) * mix_w].reshape(d_mix.shape[2:])
         sums[...] = acc[...]
 
 
-def dense(lay, tokens, att, den, cot, vectors, g_mix, g_up, g_down):
+def dense(lay, tokens, att, den, cot, vectors, w_mix, g_up, g_down, mix_shape, split):
     total, width = tokens.shape
     block = 256 if total % 256 == 0 else total
     row_blocks = total // block
     ff = g_up.shape[-1] * lay.C
     chunk = ff // lay.Z
-    up_w, down_w = g_up.shape[-1], g_down.shape[-1]
-    direct = up_w % 128 == 0 and down_w % 128 == 0
-    slots = [g.shape for g in (g_mix, g_up, g_down)]
-    if not direct:
+    up_w = g_up.shape[-1]
+    slots = [(lay.X, 2, lay.Z, lay.Y) + mix_shape, g_up.shape, g_down.shape]
+    if not split:
         g_up = g_up.transpose(2, 3, 4, 0, 1, 5).reshape(lay.Z, lay.Y, g_up.shape[4], ff)
         g_down = g_down.transpose(0, 1, 4, 2, 3, 5).reshape(lay.C, g_down.shape[4], ff)
+    starts = [0, row_blocks, 2 * row_blocks, 2 * row_blocks + lay.Z, 3 * row_blocks + lay.Z]
     last = row_blocks - 1
     per = chunk // up_w
-    by_row = pl.BlockSpec((block, width), lambda i: (jnp.minimum(i, last), 0))
+    phase = lambda i, n, size: jnp.clip(i - starts[n], 0, size - 1)
+    in_phase = lambda n, wide=width: pl.BlockSpec((block, wide), lambda i: (phase(i, n, row_blocks), 0))
+    twice = pl.BlockSpec((block, width), lambda i: (jnp.where(i < starts[1], i, phase(i, 3, row_blocks)), 0))
     fixed = lambda shape: pl.BlockSpec(shape, lambda i: (0,) * len(shape), pipeline_mode=pl.Buffered(1))
     anyspace = pl.BlockSpec(memory_space=pl.ANY)
-    later = lambda i: jnp.maximum(i - row_blocks, 0)
+    later = lambda i: phase(i, 4, lay.Z)
     if per == 1:
         up_spec = pl.BlockSpec((1, 1) + slots[1][2:], lambda i: (later(i) // 2, later(i) % 2, 0, 0, 0, 0))
     else:
         up_spec = pl.BlockSpec((per // 2, 2) + slots[1][2:], lambda i: (later(i), 0, 0, 0, 0, 0))
-    down_spec = pl.BlockSpec(slots[2][:2] + (1,) + slots[2][3:], lambda i: (0, 0, later(i), 0, 0, 0))
+    half = slots[2][:1] + slots[2][2:]
+    cuts = pieces(slots[2][4], 1)
+    if split:
+        down_shape, down_spec = half, anyspace
+    else:
+        down_shape = slots[2]
+        down_spec = pl.BlockSpec(
+            slots[2][:2] + (1,) + slots[2][3:], lambda i: (0, 0, phase(i, 2, lay.Z), 0, 0, 0)
+        )
     shape = jax.ShapeDtypeStruct
-    return pl.pallas_call(
-        functools.partial(dense_kernel, lay, row_blocks, chunk, direct),
-        grid=(row_blocks + lay.Z,),
-        out_shape=[
-            shape((total, width), BF16),
-            shape((total, width), F32),
-            shape((total, 2 * width), BF16),
-            shape((width, total), BF16),
-            shape(slots[0], BF16),
-            shape(slots[1], BF16),
-            shape(slots[2], BF16),
-            shape((4, ff), F32),
-        ],
-        in_specs=[by_row] * 4 + [fixed(v.shape) for v in vectors] + [anyspace] * 3,
-        out_specs=[
-            by_row,
-            by_row,
-            pl.BlockSpec((block, 2 * width), lambda i: (jnp.minimum(i, last), 0)),
-            pl.BlockSpec((width, block), lambda i: (0, jnp.minimum(i, last))),
-            fixed(slots[0]),
-            up_spec,
-            down_spec,
-            fixed((4, ff)),
-        ],
-        scratch_shapes=[
-            pltpu.VMEM((width, width), BF16),
-            pltpu.VMEM((lay.Z, lay.Y, slots[1][4], ff), BF16),
-            pltpu.VMEM((lay.C, slots[2][4], ff), BF16),
-            pltpu.VMEM(slots[0], BF16),
-            pltpu.VMEM((total, ff), BF16),
-            pltpu.VMEM((total, ff), BF16),
-            pltpu.VMEM((width, total), BF16),
-            pltpu.VMEM((width, total), BF16),
-            pltpu.VMEM((width, total), BF16),
-            pltpu.VMEM((total, width), BF16),
-            pltpu.VMEM((block, ff), F32),
-            pltpu.VMEM((4, ff), F32),
-            pltpu.SemaphoreType.DMA((3 + lay.C + lay.C * lay.R,)),
-        ],
-        compiler_params=pltpu.CompilerParams(vmem_limit_bytes=VMEM_LIMIT),
+    outs = [
+        shape((total, width), BF16),
+        shape((total, width), F32),
+        shape((total, 2 * width), BF16),
+        shape(slots[0], BF16),
+        shape(slots[1], BF16),
+        shape(down_shape, BF16),
+        shape((4, ff), F32),
+    ]
+    out_specs = [
+        in_phase(1), in_phase(3), in_phase(3, 2 * width), fixed(slots[0]), up_spec, down_spec, fixed((4, ff)),
+    ]
+    scratch = [
+        pltpu.VMEM((width, width), BF16),
+        pltpu.VMEM((lay.Z, lay.Y, slots[1][4], ff), BF16),
+        pltpu.VMEM((lay.C, slots[2][4], ff), BF16),
+        pltpu.VMEM((total, ff), BF16),
+        pltpu.VMEM((total, ff), BF16),
+        pltpu.VMEM((width, total), BF16),
+        pltpu.VMEM((width, total), BF16),
+        pltpu.VMEM((width, total), BF16),
+        pltpu.VMEM((total, width), BF16),
+        pltpu.VMEM((total, width), F32),
+        pltpu.VMEM((total, 128), F32),
+        pltpu.VMEM((total, width), F32),
+        pltpu.VMEM((8, ff), F32),
+        pltpu.VMEM((4, ff), F32),
+        pltpu.SemaphoreType.DMA((3 + lay.C + lay.C * lay.R,)),
+    ]
+    params = dict(vmem_limit_bytes=VMEM_LIMIT)
+    aliases = {}
+    if split:
+        outs.append(shape(slots[2], BF16))
+        out_specs.append(anyspace)
+        aliases = {13: 7}
+        scratch += [pltpu.VMEM(slots[2], BF16), pltpu.VMEM(half, BF16)]
+        for _, n, y_first in cuts:
+            tile = (n, slots[2][5])
+            first = (lay.Y - 1, lay.X, lay.Z) if y_first else (lay.X - 1, lay.Z, lay.Y)
+            scratch.append(pltpu.VMEM(first + tile, BF16))
+        scratch += [pltpu.SemaphoreType.DMA((len(cuts) * lay.hops,))] * 4
+        params.update(collective_id=2, has_side_effects=True)
+    results = pl.pallas_call(
+        functools.partial(dense_kernel, lay, row_blocks, chunk, split, cuts),
+        grid=(3 * row_blocks + 2 * lay.Z,),
+        out_shape=outs,
+        in_specs=[in_phase(0), twice, in_phase(3), in_phase(1)] + [fixed(v.shape) for v in vectors] + [anyspace] * 3,
+        out_specs=out_specs,
+        scratch_shapes=scratch,
+        input_output_aliases=aliases,
+        compiler_params=pltpu.CompilerParams(**params),
         name="dense",
-    )(tokens, att, den, cot, *vectors, g_mix, g_up, g_down)
+    )(tokens, att, den, cot, *vectors, w_mix, g_up, g_down)
+    return results[:7]
 
 
 class Scatter:
@@ -742,6 +891,11 @@
             self.own_copy().start()
 
     def advance(self, number):
+        self.add(number)
+        if number < 4:
+            self.start(number)
+
+    def add(self, number):
         p, rows, lay, mine = self.p, self.rows, self.p.lay, self.mine
         if number == 1 and self.fetch is not None:
             self.own_copy().wait()
@@ -789,25 +943,24 @@
             for d in range(lay.Z - 1):
                 total = total + self.fourth[d].astype(F32)
             self.target[rows, :] = total
-            return
-        self.start(number)
-
-    def sent(self):
-        for number in range(4):
+
+    def sent(self, numbers):
+        for number in numbers:
             for copy in self.stage(number):
                 copy.wait_send()
 
 
 def backward_kernel(
-    lay, seqs, length, cuts, *refs
+    lay, seqs, length, cuts, split, *refs
 ):
     (carry, ids, prev, tok_t, sums, q_hbm, k_hbm, v_hbm, given_hbm, full_in, pre, d_mix, d_up, d_down) = refs[:14]
     (tokens_grad, o_in, o_mix, o_up, o_down, o_sums) = refs[14:20]
     rest = list(refs[20:])
     (mask, tab, out_state, in_state, flags, key_part, value_part, grads, held, given_in, d_in, vec, vec_in,
-     mine_mix, mine_up, mine_down, came_mix, came_up, came_down, came_in) = rest[:20]
+     mine_mix, mine_up, mine_down, came_mix, came_up, came_in) = rest[:19]
     send, recv, misc_send, misc_recv, local = rest[-5:]
-    landing = rest[20:-5]
+    came_down = None if split else rest[19]
+    landing = rest[19 if split else 20 : -5]
     p = Place(lay)
     _, total_rows, width = held.shape
     q_in, k_in, v_in = held.at[0], held.at[1], held.at[2]
@@ -841,9 +994,16 @@
             base += lay.hops
             used += 1
         groups.append(group)
-    for group in groups[:3]:
+    if split:
+        down_copy = pltpu.make_async_copy(d_down, mine_down, local.at[0])
+        down_copy.start()
+    for group in groups[1 if split else 0 : 3]:
         for flow in group:
             flow.begin()
+    if split:
+        down_copy.wait()
+        for flow in groups[0]:
+            flow.start(2)
 
     def pre_copy(b):
         return pltpu.make_async_copy(pre.at[pl.ds(b * 256, 256)], key_part.at[pl.ds(b * 256, 256)], misc_recv.at[2 + b])
@@ -931,24 +1091,30 @@
         def _():
             chain_copy().start()
 
-    def line(number, group):
-        return [functools.partial(flow.advance, number) for flow in groups[group]]
-
-    order = [(1, 0), (1, 1), (2, 0), (1, 2), (2, 1), (3, 0), (2, 2), (3, 1), (4, 0), (3, 2), (4, 1), (4, 2)]
-    thunks = [thunk for number, group in order for thunk in line(number, group)]
-    inside = (len(thunks) * 2) // 3
+    def onward(number, group):
+        for flow in groups[group]:
+            flow.advance(number)
+
+    back = lay.C - 1 - p.c
+    pl.when(back == 0)(chain_step)
+    pl.when(back == 1)(chain_step)
+    for group in (1, 2) if split else (0, 1):
+        onward(1, group)
+    chain_turn = (total * 2) // 3 + ((back - 2) * (total // 3)) // max(lay.C - 2, 1)
+
+    during = [(1, 3, 0), (7, 2, 1), (9, 2, 2), (10, 4, 0)] if split else [(0, 1, 2), (3, 2, 0), (7, 2, 1), (9, 3, 0)]
     block = 256 if length % 256 == 0 else length
 
     def local_attention(it, _):
-        @pl.when(it == ((lay.C - 1 - p.c) * total) // lay.C)
+        @pl.when((it == chain_turn) & (back > 1))
         def _():
             chain_step()
 
-        for n, thunk in enumerate(thunks[:inside]):
-
-            @pl.when(it == (n * total) // inside)
-            def _(thunk=thunk):
-                thunk()
+        for turn, number, group in during:
+
+            @pl.when(it == (turn * total) // 12)
+            def _(number=number, group=group):
+                onward(number, group)
 
         s, rows, lanes = where(it)
         for seq in range(seqs):
@@ -1026,6 +1192,8 @@
         return 0
 
     lax.fori_loop(0, total, finish, 0)
+    for number, group in [(3, 1), (3, 2)] if split else [(2, 2), (4, 0), (3, 1), (3, 2)]:
+        onward(number, group)
     for b in range(blocks):
         pre_copy(b).start()
     thirds = [
@@ -1094,15 +1262,9 @@
             vector_start(number + 1)
 
     vector_start(0)
-    for thunk in thunks[inside:]:
-        thunk()
-    tail = []
-    for number in (1, 2, 3, 4):
-        tail += line(number, 3)
-        tail.append(functools.partial(vector_add, number - 1))
-    done = 0
     for copy in thirds:
         copy.wait()
+    after = [[(1, 3)], [(4, 1), (4, 2)], [], []]
     for b in range(blocks):
         pre_copy(b).wait()
         part = slice(b * 256, (b + 1) * 256)
@@ -1111,17 +1273,20 @@
             out = out + dot(grads[part, i * width : (i + 1) * width], held[i, 0:width, :], NT)
         value_part[part, :] = out
         grad_copy(b).start()
-        upto = (len(tail) * (b + 1)) // (blocks + 1)
-        for thunk in tail[done:upto]:
-            thunk()
-        done = upto
-    for thunk in tail[done:]:
-        thunk()
+        for number, group in after[b] if b < len(after) else []:
+            onward(number, group)
+    vector_add(0)
+    onward(2, 3)
+    vector_add(1)
+    onward(3, 3)
+    vector_add(2)
+    onward(4, 3)
+    vector_add(3)
     for b in range(blocks):
         grad_copy(b).wait()
     for group in groups:
         for flow in group:
-            flow.sent()
+            flow.sent(range(2, 4) if split and group is groups[0] else range(4))
     for number in range(4):
         for copy in vector_stage(number):
             copy.wait_send()
@@ -1131,19 +1296,22 @@
         chain_copy().wait_send()
 
 
-def backward(lay, ids, prev, q, k, v, given, carry, tok_t, full_in, sums, pre, d_mix, d_up, d_down, in_shape):
+def backward(
+    lay, ids, prev, q, k, v, given, carry, tok_t, full_in, sums, pre, d_mix, d_up, d_down, shapes, split
+):
     seqs, length = ids.shape
     rows, width = q.shape
     total = seqs * (width // 128)
-    in_slots = (lay.X, 2, lay.Z, lay.Y) + in_shape
-    sources = (d_down, d_up, d_mix, in_slots)
-    slots = [s if isinstance(s, tuple) else s.shape for s in sources]
-    cuts = tuple(pieces(s[4], 1) for s in slots)
+    slots = [(lay.X, 2, lay.Z, lay.Y) + s for s in shapes]
+    in_slots = slots[3]
+    cuts = tuple(pieces(s[4], n) for s, n in zip(slots, (1, 1, 1, 3), strict=True))
     landing = []
-    for slot, parts in zip(slots, cuts, strict=True):
+    for index, (slot, parts) in enumerate(zip(slots, cuts, strict=True)):
         for _, n, y_first in parts:
             tile = (n, slot[5])
-            if y_first:
+            if split and index == 0:
+                landing += [(1, 1, 1, 16, 128), ((lay.X if y_first else lay.Y) - 1, lay.Z) + tile]
+            elif y_first:
                 landing += [(lay.Y - 1, lay.X, lay.Z) + tile, (lay.X - 1, lay.Z) + tile]
             else:
                 landing += [(lay.X - 1, lay.Z, lay.Y) + tile, (lay.Y - 1, lay.Z) + tile]
@@ -1171,7 +1339,7 @@
         pltpu.VMEM((4, 4, ff), F32),
         pltpu.VMEM((hop, 4, ff), F32),
     ]
-    scratch += [pltpu.VMEM(half[i], BF16) for i in (2, 1, 0)] + [pltpu.VMEM(half[i], BF16) for i in (2, 1, 0, 3)]
+    scratch += [pltpu.VMEM(half[i], BF16) for i in (2, 1, 0)] + [pltpu.VMEM(half[i], BF16) for i in ((2, 1, 3) if split else (2, 1, 3, 0))]
     scratch += [pltpu.VMEM(s, BF16) for s in landing]
     scratch += [
         pltpu.SemaphoreType.DMA((flows * hop,)),
@@ -1181,7 +1349,7 @@
         pltpu.SemaphoreType.DMA((flows + 4,)),
     ]
     return pl.pallas_call(
-        functools.partial(backward_kernel, lay, seqs, length, cuts),
+        functools.partial(backward_kernel, lay, seqs, length, cuts, split),
         out_shape=[shape((rows, width), F32)]
         + [shape(slots[i][4:], F32) for i in (3, 2, 1, 0)]
         + [shape((4, ff), F32)],
@@ -1195,6 +1363,46 @@
     )(carry, ids, prev, tok_t, sums, q, k, v, given, full_in, pre, d_mix, d_up, d_down)
 
 
+def finish_kernel(tok_in, layer_in, in_in, mix_in, up_in, down_in, sums, *outs):
+    layer_out, tokens_grad, o_in, in_b, o_mix, mix_b, gain1, shift1, o_up, up_b, o_down, down_b, gain2, shift2 = outs
+    width = tok_in.shape[1]
+    layer_out[...] = layer_in[...]
+    tokens_grad[...] = tok_in[...]
+
+    @pl.when(pl.program_id(0) == 0)
+    def _():
+        o_in[...] = in_in[...]
+        o_mix[...] = mix_in[...]
+        o_up[...] = up_in[...]
+        o_down[...] = jnp.transpose(down_in[...])
+        for out, row, at in (
+            (up_b, 0, 0), (in_b, 1, 0), (mix_b, 2, 0), (gain1, 2, 1), (shift1, 2, 2), (down_b, 2, 3), (gain2, 3, 0), (shift2, 3, 1),
+        ):
+            size = out.shape[0]
+            out[...] = sums[row : row + 1, at * width : at * width + size].reshape(size)
+
+
+def finish_all(tokens_grad, layer_out, o_in, o_mix, o_up, o_down, sums):
+    rows, width = tokens_grad.shape
+    ff = sums.shape[1]
+    block = 256 if rows % 256 == 0 else rows
+    by_row = pl.BlockSpec((block, width), lambda i: (i, 0))
+    fixed = lambda shape: pl.BlockSpec(shape, lambda i: (0,) * len(shape))
+    sizes = [
+        None, None, o_in.shape, (3 * width,), o_mix.shape, (width,), (width,), (width,), o_up.shape, (ff,),
+        o_down.shape[::-1], (width,), (width,), (width,),
+    ]
+    shape = jax.ShapeDtypeStruct
+    return pl.pallas_call(
+        finish_kernel,
+        grid=(rows // block,),
+        out_shape=[shape((rows, width), BF16), shape((rows, width), F32)] + [shape(n, F32) for n in sizes[2:]],
+        in_specs=[by_row] * 2 + [fixed(a.shape) for a in (o_in, o_mix, o_up, o_down, sums)],
+        out_specs=[by_row] * 2 + [fixed(n) for n in sizes[2:]],
+        name="finish",
+    )(tokens_grad, layer_out, o_in, o_mix, o_up, o_down, sums)
+
+
 def per_device(
     tokens, segment_ids, in_weight, in_bias, mix_weight, mix_bias, first_gain, first_shift,
     up_weight, up_bias, down_weight, down_bias, second_gain, second_shift, cotangent,
@@ -1202,35 +1410,22 @@
     lay = Layout(lax.axis_size("row"), lax.axis_size("col"))
     seqs, length, width = tokens.shape
     flat = tokens.reshape(seqs * length, width)
-    line = lambda v: v.astype(F32)[None]
-    q, k, v, att, den, carry, prev, full_in, g_mix, g_up, g_down = forward(
-        lay, flat, segment_ids, line(in_bias), (in_weight, mix_weight, up_weight, down_weight.T)
+    split = up_weight.shape[1] % 128 == 0 and down_weight.shape[0] % 128 == 0
+    shards = (in_weight, mix_weight, up_weight, down_weight.T)
+    att, den, carry, prev, q, k, v, full_in, full_mix, tok_t, g_up, g_down = forward(
+        lay, flat, segment_ids, in_bias, shards, split
     )
-    vectors = [line(u) for u in (mix_bias, up_bias, down_bias, first_gain, first_shift, second_gain, second_shift)]
-    layer_out, pre, given, tok_t, d_mix, d_up, d_down, sums = dense(
-        lay, flat, att, den, cotangent.reshape(seqs * length, width), vectors, g_mix, g_up, g_down
+    vectors = (up_bias, mix_bias, down_bias, first_gain, first_shift, second_gain, second_shift)
+    layer_out, pre, given, d_mix, d_up, d_down, sums = dense(
+        lay, flat, att, den, cotangent.reshape(seqs * length, width), vectors, full_mix, g_up, g_down,
+        mix_weight.shape, split,
     )
     tokens_grad, o_in, o_mix, o_up, o_down, o_sums = backward(
         lay, segment_ids, prev, q, k, v, given, carry, tok_t, full_in, sums, pre, d_mix, d_up, d_down,
-        in_weight.shape,
+        [shards[i].shape for i in (3, 2, 1, 0)], split,
     )
-    part = lambda row, n: o_sums[row, n * width : (n + 1) * width]
-    return (
-        layer_out.reshape(tokens.shape),
-        tokens_grad.reshape(tokens.shape),
-        o_in,
-        o_sums[1, : 3 * width],
-        o_mix,
-        part(2, 0),
-        part(2, 1),
-        part(2, 2),
-        o_up,
-        o_sums[0],
-        o_down.T,
-        part(2, 3),
-        part(3, 0),
-        part(3, 1),
-    )
+    outs = finish_all(tokens_grad, layer_out, o_in, o_mix, o_up, o_down, o_sums)
+    return (outs[0].reshape(tokens.shape), outs[1].reshape(tokens.shape), *outs[2:])
 
 
 def solution(mesh):

time: 320 us -> 276 us (0.86)
  Pallas kernels: 297 us -> 273 us
  local copies, waits for them, and re-layouts: 19.7 us -> 1.86 us
    pallas_call x1, Pallas kernels: 120 us -> 93.4 us  [backward(): pl.pallas_call(functools.partial(backward_kernel, lay, seqs, length, cuts...]
    broadcast_in_dim x7 -> x0, local copies, waits for them, and re-layouts: 8.86 us -> none  [per_device(): line = lambda v: v.astype(F32)[None]]
    unnamed x13 -> x1, local copies, waits for them, and re-layouts: 6.61 us -> 1.86 us
    slice x3 -> x0, local copies, waits for them, and re-layouts: 4.26 us -> none  [the longest x1 1.46 us: per_device(): part = lambda row, n: o_sums[row, n * width:(n + 1) * width]]
    pallas_call x2 -> x3, Pallas kernels: 177 us -> 180 us  [the longest x1 96.9 us: dense(): pl.pallas_call(functools.partial(dense_kernel, lay, row_blocks, chunk, sp...]
where the time goes in v2:
time: 276 us; the launch traced here: 275 us
  Pallas kernels  273 us (99%)
    pallas_call x1, Pallas kernels, dense(): pl.pallas_call(functools.partial(dense_kernel, lay, row_blocks, chunk, sp...  96.9 us
    pallas_call x1, Pallas kernels, backward(): pl.pallas_call(functools.partial(backward_kernel, lay, seqs, length, cuts...  93.4 us
    pallas_call x1, Pallas kernels, forward(): pl.pallas_call(functools.partial(forward_kernel, lay, seqs, length, cuts,...  76.8 us
    pallas_call x1, Pallas kernels, finish_all(): pl.pallas_call(finish_kernel, grid=(rows // block,), out_shape=[shape((ro...  5.78 us

profile of v2, /device:TPU:0, one launch (start us, length us, event | category | flops | bytes accessed | tf_op | source)
XLA Modules:
  0.0 275.4 jit_solution(17320870297789997644)
XLA Ops:
  0.6 76.8 %forward_attention.1 = (f32[1024,768]{1,0:T(8,128)}, f32[1024,768]{1,0:T(8,128)}, bf16[12,80,256]{2,1,0:T(8,128)(2,1)}, s32[2,512]{1,0:T(2,128)}, bf16[1024,768]...) custom-call(bf16[1024,768]{1,0:T(8,128)(2,1)} %bitcast.5, ...), custom_call_target="tpu_custom_call" | custom-call | tf_op jit(solution)/shard_map/forward_attention/pallas_call | solution.py:453
  77.5 96.9 %dense.1 = (bf16[1024,768]{1,0:T(8,128)(2,1)}, f32[1024,768]{1,0:T(8,128)}, bf16[1024,1536]{1,0:T(8,128)(2,1)}, bf16[2,2,4,2,96,192]{5,4,3,2,1,0:T(8,128)(2,1)},...) custom-call(bf16[1024,768]{1,0:T(8,128)(2,1)} %bitcast.6, ...), custom_call_target="tpu_custom_call", output_to_operand_aliasing={{7}: (13, {})} | custom-call | tf_op jit(solution)/shard_map/dense/pallas_call | solution.py:829
  174.4 93.4 %backward_attention.1 = (f32[1024,768]{1,0:T(8,128)}, f32[96,576]{1,0:T(8,128)}, f32[96,192]{1,0:T(8,128)}, f32[96,768]{1,0:T(8,128)}, f32[192,384]{1,0:T(8,128)}, /*index=5*/f32[4,3072]{1,0:T(4,128)}) custom-call(bf16[12,80,256]{2,1,0:T(8,128)(2,1)} %get-tuple-element.53.refs_0_, s32[2,512]{1,0:T(2,128)} %refs_1_.1, s32[2,512]{1,0:T(2,128)} %get-tuple-element.54.refs_2_, ...), custom_call_target="tpu_custom_call" | custom-call | tf_op jit(solution)/shard_map/backward_attention/pallas_call | solution.py:1351
  267.8 5.8 %finish.1 = (bf16[1024,768]{1,0:T(8,128)(2,1)}, f32[1024,768]{1,0:T(8,128)}, f32[96,576]{1,0:T(8,128)}, f32[2304]{0:T(1024)}, f32[96,192]{1,0:T(8,128)}, /*index...) custom-call(f32[1024,768]{1,0:T(8,128)} %get-tuple-element.71.tok_in, ...), custom_call_target="tpu_custom_call" | custom-call | tf_op jit(solution)/shard_map/finish/pallas_call | solution.py:1396
  273.6 1.9 copy.30

commit v3 on v2

--- a/solution.py
+++ b/solution.py
@@ -269,40 +269,34 @@
         tab[s, 3] = sin_e * last_mask
         flags[s] = jnp.broadcast_to(passes, (8, 256))
 
-    for number in (2, 3):
-        for flow in groups[0]:
+    def go(number, some):
+        for flow in some:
             flow.advance(number)
-    for flow in groups[0]:
+
+    ins, mixes, ups, downs = groups
+    go(2, ins)
+    go(1, mixes)
+    go(3, ins)
+    go(1, ups[:2])
+    for flow in ins:
         flow.arrive(3)
-
-    def onward(number, group):
-        for flow in groups[group]:
-            flow.advance(number)
-
-    onward(1, 1)
+    go(2, mixes)
     unslot(g_in, full_in, lay, in_s.shape[0], in_s.shape[1], False)
     outputs[3].start()
-
-    blocks = width // 256
     half = tokens.shape[0] // 2
 
     def project(target, start, relu):
-        def column_block(j, _):
-            lanes = pl.ds(pl.multiple_of(j * 256, 256), 256)
-            source = pl.ds(pl.multiple_of(start + j * 256, 256), 256)
-            for m in range(2):
-                out = dot(tokens[m * half : (m + 1) * half, :], full_in[:, source]) + bias[:, source]
-                if relu:
-                    out = jnp.maximum(out, 0.0)
-                target[m * half : (m + 1) * half, lanes] = out.astype(BF16)
-            return 0
-
-        lax.fori_loop(0, blocks, column_block, 0)
+        for m in range(2):
+            rows = slice(m * half, (m + 1) * half)
+            out = dot(tokens[rows, :], full_in[:, start : start + width]) + bias[:, start : start + width]
+            if relu:
+                out = jnp.maximum(out, 0.0)
+            target[rows, :] = out.astype(BF16)
 
     project(k_out, width, True)
-    onward(1, 2)
+    go(1, ups[2:])
+    go(2, ups[:2])
     project(v_out, 2 * width, False)
-    during = [(2, 1), (2, 2), (3, 1)] if split else [(2, 1), (2, 2), (1, 3), (3, 1)]
 
     def where(it):
         s, pair = it // pairs, it % pairs
@@ -360,6 +354,7 @@
     for copy in outputs[:3]:
         copy.start()
     pl.when(p.c == 1)(chain_step)
+    go(2, ups[2:])
     step_block = 256 if length % 256 == 0 else length
     chain_turn = (total * 2) // 3 + ((p.c - 2) * (total // 3)) // max(lay.C - 2, 1)
 
@@ -368,11 +363,11 @@
         def _():
             chain_step()
 
-        for n, (number, group) in enumerate(during):
-
-            @pl.when(it == (n * total) // len(during))
-            def _(number=number, group=group):
-                onward(number, group)
+        for turn, number, some in ((3, 3, mixes), (5, 3, ups[:2]), (8, 1, downs)):
+
+            @pl.when(it == (turn * total) // 12)
+            def _(number=number, some=some):
+                go(number, some)
 
         s, rows, lanes = where(it)
         low, high = lane_half(0), lane_half(1)
@@ -413,8 +408,9 @@
         return 0
 
     lax.fori_loop(0, total, finish, 0)
-    for number, group in [(3, 2)] if split else [(3, 2), (2, 3), (3, 3)]:
-        onward(number, group)
+    go(3, ups[2:])
+    for number in () if split else (2, 3):
+        go(number, downs)
     for flow in groups[1]:
         flow.arrive(3)
     unslot(g_mix, full_mix, lay, mix_s.shape[0], mix_s.shape[1], False)
@@ -422,9 +418,9 @@
     for flow in groups[2]:
         flow.arrive(3)
     for flow in groups[3]:
-        flow.arrive(0 if split else 3)
+        flow.arrive(1 if split else 3)
     for flow in flows:
-        flow.sent(range(1) if split and flow in groups[3] else range(4))
+        flow.sent(range(2) if split and flow in groups[3] else range(4))
     ring_ids.wait_send()
     for copy in outputs:
         copy.wait()
@@ -438,7 +434,7 @@
     seqs, length = ids.shape
     rows, width = tokens.shape
     total = seqs * (width // 128)
-    cuts = [pieces(s.shape[0], n) for s, n in zip(shards, (3, 1, 1, 1), strict=True)]
+    cuts = [pieces(s.shape[0], n) for s, n in zip(shards, (3, 1, 2, 2), strict=True)]
     cuts = tuple(cuts)
     flows = sum(len(c) for c in cuts)
     vmem, anyspace = pl.BlockSpec(memory_space=pltpu.VMEM), pl.BlockSpec(memory_space=pl.ANY)
@@ -496,7 +492,7 @@
 
 
 def dense_kernel(
-    lay, row_blocks, chunk, split, cuts, *refs
+    lay, row_blocks, chunk, split, gather_cuts, cuts, *refs
 ):
     tokens, att, den, cot = refs[:4]
     given_vectors = refs[4:11]
@@ -509,7 +505,6 @@
     step = pl.program_id(0)
     block, width = tokens.shape
     ff = act.shape[1]
-    chunks = ff // chunk
     mix_w, up_w = d_mix.shape[-1], d_up.shape[-1]
     down_a, down_w = g_down.shape[-2:] if split else d_down_out.shape[-2:]
     mix_b, down_b, gain1, shift1, gain2, shift2 = [vectors.at[i : i + 1, 0:width] for i in range(1, 7)]
@@ -545,8 +540,9 @@
         send, recv, send2, recv2 = rest[-4:]
         p = Place(lay)
         gathers, scatters = [], []
+        for n, (r0, size, y_first) in enumerate(gather_cuts):
+            gathers.append(Gather(p, None, g_down, r0, size, y_first, send, recv, n * lay.hops))
         for n, (r0, size, y_first) in enumerate(cuts):
-            gathers.append(Gather(p, None, g_down, r0, size, y_first, send, recv, n * lay.hops))
             scatters.append(
                 Scatter(
                     p, d_down, d_down.at[:, p.k], came, landing[n], None, None, None,
@@ -555,11 +551,7 @@
             )
         out_copy = pltpu.make_async_copy(d_down.at[:, p.k], d_down_out, sem.at[1])
 
-    def up_chunk(lanes):
-        return w_up[:, :, :, lanes].reshape(width, chunk)
-
-    def down_chunk(lanes):
-        return w_down[:, :, lanes].reshape(width, chunk)
+    wide = 2 * chunk if ff % (2 * chunk) == 0 else chunk
 
     @pl.when(step == 0)
     def _():
@@ -568,7 +560,7 @@
         if split:
             p.barrier()
             for flow in gathers:
-                flow.start(1)
+                flow.start(2)
         for i, vector in enumerate(given_vectors):
             vectors[i : i + 1, 0 : vector.shape[0]] = vector[...].astype(F32).reshape(1, vector.shape[0])
         acc[...] = jnp.zeros_like(acc)
@@ -593,27 +585,23 @@
                 copy.wait()
 
         def up_part(n, _):
-            lanes = pl.ds(pl.multiple_of(n * chunk, chunk), chunk)
-            up = dot(hidden_low, up_chunk(lanes)) + vectors[0:1, lanes]
+            lanes = pl.ds(pl.multiple_of(n * wide, wide), wide)
+            up = dot(hidden_low, w_up[:, :, :, lanes].reshape(width, wide)) + vectors[0:1, lanes]
             cdf = 0.5 + 0.5 * lax.erf(up * math.sqrt(0.5))
             density = jnp.exp(up * up * -0.5) * (1.0 / math.sqrt(2.0 * math.pi))
             up_g[rows, lanes] = (cdf + up * density).astype(BF16)
             act[rows, lanes] = (up * cdf).astype(BF16)
             if split:
-
-                @pl.when((step == 1) & (n == 1))
-                def _():
-                    for flow in gathers:
-                        flow.advance(2)
-
-                @pl.when((step == starts[1] - 1) & (n == 1))
-                def _():
-                    for flow in gathers:
-                        flow.advance(3)
+                for turn, some in ((2, gathers[:2]), (3, gathers[2:])):
+
+                    @pl.when((step == (turn * row_blocks) // 4) & (n == turn - 2))
+                    def _(some=some):
+                        for flow in some:
+                            flow.advance(3)
 
             return 0
 
-        lax.fori_loop(0, chunks, up_part, 0)
+        lax.fori_loop(0, ff // wide, up_part, 0)
 
     if split:
 
@@ -633,11 +621,7 @@
     def _():
         rows = pl.ds(pl.multiple_of((step - starts[1]) * block, block), block)
 
-        def down_part(n, total):
-            lanes = pl.ds(pl.multiple_of(n * chunk, chunk), chunk)
-            return total + dot(act[rows, lanes], down_chunk(lanes), NT)
-
-        down = lax.fori_loop(0, chunks, down_part, jnp.zeros((block, width), F32)) + down_b[...]
+        down = dot(act[rows, :], w_down[...].reshape(width, ff), NT) + down_b[...]
         hidden = unit_v[rows, :] * gain1[...] + shift1[...]
         unit2, scale2 = normalize(hidden + down)
         layer_out[...] = (unit2 * gain2[...] + shift2[...]).astype(BF16)
@@ -681,7 +665,7 @@
                 flow.add(2)
             out_copy.start()
             for flow in gathers:
-                flow.sent(range(1, 4))
+                flow.sent(range(2, 4))
             for flow in scatters:
                 flow.sent(range(2))
             out_copy.wait()
@@ -692,14 +676,16 @@
         sum_grad = grad_v[rows, :]
         down_grad = sum_grad.astype(BF16)
 
-        def back(n, total):
-            lanes = pl.ds(pl.multiple_of(n * chunk, chunk), chunk)
-            grad = (dot(down_grad, down_chunk(lanes)) * up_g[rows, lanes].astype(F32)).astype(BF16)
+        def back(n, _):
+            lanes = pl.ds(pl.multiple_of(n * wide, wide), wide)
+            grad = dot(down_grad, w_down[:, :, lanes].reshape(width, wide)) * up_g[rows, lanes].astype(F32)
+            grad = grad.astype(BF16)
             up_g[rows, lanes] = grad
             acc[0:1, lanes] += rows_sum(grad.astype(F32))
-            return total + dot(grad, up_chunk(lanes), NT)
-
-        hidden_grad = lax.fori_loop(0, chunks, back, sum_grad)
+            return 0
+
+        lax.fori_loop(0, ff // wide, back, 0)
+        hidden_grad = sum_grad + dot(up_g[rows, :], w_up[...].reshape(width, ff), NT)
         unit1, scale1 = unit_v[rows, :], scale_v[rows, 0:1]
         acc[2:3, width : 2 * width] += rows_sum(hidden_grad * unit1)
         acc[2:3, 2 * width : 3 * width] += rows_sum(hidden_grad)
@@ -775,7 +761,7 @@
     else:
         up_spec = pl.BlockSpec((per // 2, 2) + slots[1][2:], lambda i: (later(i), 0, 0, 0, 0, 0))
     half = slots[2][:1] + slots[2][2:]
-    cuts = pieces(slots[2][4], 1)
+    gather_cuts, cuts = pieces(slots[2][4], 2), pieces(slots[2][4], 1)
     if split:
         down_shape, down_spec = half, anyspace
     else:
@@ -824,10 +810,11 @@
             tile = (n, slots[2][5])
             first = (lay.Y - 1, lay.X, lay.Z) if y_first else (lay.X - 1, lay.Z, lay.Y)
             scratch.append(pltpu.VMEM(first + tile, BF16))
-        scratch += [pltpu.SemaphoreType.DMA((len(cuts) * lay.hops,))] * 4
+        for n in (gather_cuts, gather_cuts, cuts, cuts):
+            scratch.append(pltpu.SemaphoreType.DMA((len(n) * lay.hops,)))
         params.update(collective_id=2, has_side_effects=True)
     results = pl.pallas_call(
-        functools.partial(dense_kernel, lay, row_blocks, chunk, split, cuts),
+        functools.partial(dense_kernel, lay, row_blocks, chunk, split, gather_cuts, cuts),
         grid=(3 * row_blocks + 2 * lay.Z,),
         out_shape=outs,
         in_specs=[in_phase(0), twice, in_phase(3), in_phase(1)] + [fixed(v.shape) for v in vectors] + [anyspace] * 3,
@@ -962,8 +949,8 @@
     came_down = None if split else rest[19]
     landing = rest[19 if split else 20 : -5]
     p = Place(lay)
-    _, total_rows, width = held.shape
-    q_in, k_in, v_in = held.at[0], held.at[1], held.at[2]
+    total_rows, width = key_part.shape
+    q_in, k_in, v_in = [held.at[:, pl.ds(i * width, width)] for i in range(3)]
     pairs = width // 128
     total = seqs * pairs
     spot = local.shape[0] - 4
@@ -1102,7 +1089,7 @@
         onward(1, group)
     chain_turn = (total * 2) // 3 + ((back - 2) * (total // 3)) // max(lay.C - 2, 1)
 
-    during = [(1, 3, 0), (7, 2, 1), (9, 2, 2), (10, 4, 0)] if split else [(0, 1, 2), (3, 2, 0), (7, 2, 1), (9, 3, 0)]
+    during = [(1, 3, 0), (9, 2, 1), (10, 4, 0), (11, 2, 2)] if split else [(0, 1, 2), (3, 2, 0), (7, 2, 1), (9, 3, 0)]
     block = 256 if length % 256 == 0 else length
 
     def local_attention(it, _):
@@ -1196,14 +1183,8 @@
         onward(number, group)
     for b in range(blocks):
         pre_copy(b).start()
-    thirds = [
-        pltpu.make_async_copy(
-            full_in.at[:, pl.ds(i * width, width)], held.at[i, pl.ds(0, width)], local.at[spot + i]
-        )
-        for i in range(3)
-    ]
-    for copy in thirds:
-        copy.start()
+    weight_copy = pltpu.make_async_copy(full_in, held.at[pl.ds(0, width)], local.at[spot])
+    weight_copy.start()
     vec[0] = sums[...]
 
     def bias_sum(n, _):
@@ -1215,21 +1196,18 @@
 
     in_a, in_w = o_in.shape
     piece = math.lcm(in_w, 128)
-    for n in range(3 * width // piece):
-        for m in range(width // 256):
-            part = dot(tok_t[m * 256 : (m + 1) * 256, :], grads[:, n * piece : (n + 1) * piece]).astype(BF16)
+
+    def in_gradient(some):
+        r0, n = some[0].r0, sum(flow.n for flow in some)
+        left = jnp.concatenate([tok_t[r * in_a + r0 : r * in_a + r0 + n, :] for r in range(lay.R)], axis=0)
+        for m in range(3 * width // piece):
+            part = dot(left, grads[:, m * piece : (m + 1) * piece]).astype(BF16)
             for i in range(piece // in_w):
-                c = n * (piece // in_w) + i
-                lo = m * 256
-                while lo < (m + 1) * 256:
-                    r = lo // in_a
-                    hi = min((r + 1) * in_a, (m + 1) * 256)
-                    d_in[c // 2, c % 2, r // lay.Y, r % lay.Y, lo - r * in_a : hi - r * in_a, :] = part[
-                        lo - m * 256 : hi - m * 256, i * in_w : (i + 1) * in_w
-                    ]
-                    lo = hi
-    for flow in groups[3]:
-        flow.begin()
+                c = m * (piece // in_w) + i
+                tile = part[:, i * in_w : (i + 1) * in_w].reshape(lay.Z, lay.Y, n, in_w)
+                d_in[c // 2, c % 2, :, :, r0 : r0 + n, :] = tile
+        for flow in some:
+            flow.begin()
 
     def vector_stage(number):
         first = (0, 1, lay.X, lay.X + lay.Y - 1)[number]
@@ -1261,27 +1239,43 @@
             vec[number + 1] = total_vec
             vector_start(number + 1)
 
-    vector_start(0)
-    for copy in thirds:
-        copy.wait()
-    after = [[(1, 3)], [(4, 1), (4, 2)], [], []]
-    for b in range(blocks):
+    def tokens_block(b):
         pre_copy(b).wait()
         part = slice(b * 256, (b + 1) * 256)
-        out = key_part[part, :]
-        for i in range(3):
-            out = out + dot(grads[part, i * width : (i + 1) * width], held[i, 0:width, :], NT)
-        value_part[part, :] = out
+        value_part[part, :] = key_part[part, :] + dot(grads[part, :], held[0:width, :], NT)
         grad_copy(b).start()
-        for number, group in after[b] if b < len(after) else []:
-            onward(number, group)
-    vector_add(0)
-    onward(2, 3)
-    vector_add(1)
-    onward(3, 3)
-    vector_add(2)
-    onward(4, 3)
+
+    def go(number, some):
+        for flow in some:
+            flow.advance(number)
+
+    ins = [groups[3][i : i + 2] for i in range(0, len(groups[3]), 2)]
+    while len(ins) < 3:
+        ins.append([])
+    vector_start(0)
+    for n in range(3):
+        if ins[n]:
+            in_gradient(ins[n])
+        vector_add(n)
+        if n:
+            go(1, ins[n - 1])
+    weight_copy.wait()
+    tokens_block(0)
+    go(1, ins[2])
+    go(2, ins[0])
     vector_add(3)
+    for b in range(1, blocks):
+        tokens_block(b)
+        if b == 1:
+            go(2, ins[1])
+    go(2, ins[2])
+    go(3, ins[0])
+    go(3, ins[1])
+    go(3, ins[2])
+    onward(4, 1)
+    onward(4, 2)
+    for some in ins:
+        go(4, some)
     for b in range(blocks):
         grad_copy(b).wait()
     for group in groups:
@@ -1333,7 +1327,7 @@
         pltpu.VMEM((rows, width), F32),
         pltpu.VMEM((rows, width), F32),
         pltpu.VMEM((rows, 3 * width), BF16),
-        pltpu.VMEM((3, rows, width), BF16),
+        pltpu.VMEM((rows, 3 * width), BF16),
         pltpu.VMEM((rows, 2 * width), BF16),
         pltpu.VMEM(in_slots, BF16),
         pltpu.VMEM((4, 4, ff), F32),

time: 276 us -> 248 us (0.90)
  Pallas kernels: 273 us -> 245 us
    pallas_call x1, Pallas kernels: 96.9 us -> 77.1 us  [dense(): pl.pallas_call(functools.partial(dense_kernel, lay, row_blocks, chunk, sp...]
    pallas_call x1, Pallas kernels: 93.4 us -> 84.7 us  [backward(): pl.pallas_call(functools.partial(backward_kernel, lay, seqs, length, cuts...]
where the time goes in v3:
time: 248 us
  Pallas kernels  245 us (99%)
    pallas_call x1, Pallas kernels, backward(): pl.pallas_call(functools.partial(backward_kernel, lay, seqs, length, cuts...  84.7 us
    pallas_call x1, Pallas kernels, forward(): pl.pallas_call(functools.partial(forward_kernel, lay, seqs, length, cuts,...  77.5 us
    pallas_call x1, Pallas kernels, dense(): pl.pallas_call(functools.partial(dense_kernel, lay, row_blocks, chunk, sp...  77.1 us
    pallas_call x1, Pallas kernels, finish_all(): pl.pallas_call(finish_kernel, grid=(rows // block,), out_shape=[shape((ro...  5.78 us

profile of v3, /device:TPU:0, one launch (start us, length us, event | category | flops | bytes accessed | tf_op | source)
XLA Modules:
  0.0 247.5 jit_solution(14747935653478877710)
XLA Ops:
  0.6 77.5 %forward_attention.1 = (f32[1024,768]{1,0:T(8,128)}, f32[1024,768]{1,0:T(8,128)}, bf16[12,80,256]{2,1,0:T(8,128)(2,1)}, s32[2,512]{1,0:T(2,128)}, bf16[1024,768]...) custom-call(bf16[1024,768]{1,0:T(8,128)(2,1)} %bitcast.5, ...), custom_call_target="tpu_custom_call" | custom-call | tf_op jit(solution)/shard_map/forward_attention/pallas_call | solution.py:449
  78.1 77.1 %dense.1 = (bf16[1024,768]{1,0:T(8,128)(2,1)}, f32[1024,768]{1,0:T(8,128)}, bf16[1024,1536]{1,0:T(8,128)(2,1)}, bf16[2,2,4,2,96,192]{5,4,3,2,1,0:T(8,128)(2,1)},...) custom-call(bf16[1024,768]{1,0:T(8,128)(2,1)} %bitcast.6, ...), custom_call_target="tpu_custom_call", output_to_operand_aliasing={{7}: (13, {})} | custom-call | tf_op jit(solution)/shard_map/dense/pallas_call | solution.py:816
  155.2 84.7 %backward_attention.1 = (f32[1024,768]{1,0:T(8,128)}, f32[96,576]{1,0:T(8,128)}, f32[96,192]{1,0:T(8,128)}, f32[96,768]{1,0:T(8,128)}, f32[192,384]{1,0:T(8,128)}, /*index=5*/f32[4,3072]{1,0:T(4,128)}) custom-call(bf16[12,80,256]{2,1,0:T(8,128)(2,1)} %get-tuple-element.53.refs_0_, s32[2,512]{1,0:T(2,128)} %refs_1_.1, s32[2,512]{1,0:T(2,128)} %get-tuple-element.54.refs_2_, ...), custom_call_target="tpu_custom_call" | custom-call | tf_op jit(solution)/shard_map/backward_attention/pallas_call | solution.py:1345
  239.9 5.8 %finish.1 = (bf16[1024,768]{1,0:T(8,128)(2,1)}, f32[1024,768]{1,0:T(8,128)}, f32[96,576]{1,0:T(8,128)}, f32[2304]{0:T(1024)}, f32[96,192]{1,0:T(8,128)}, /*index...) custom-call(f32[1024,768]{1,0:T(8,128)} %get-tuple-element.71.tok_in, ...), custom_call_target="tpu_custom_call" | custom-call | tf_op jit(solution)/shard_map/finish/pallas_call | solution.py:1390
  245.7 1.9 copy.30
